TPU v7x, 32 devices: a whole 2x2x4 slice. The times are simulated.
32 devices in a mesh: row: 8 (over z, y), col: 4 (over x, core).
Axes of the slice: x: 2, y: 2, z: 4, core: 2. Of those that a mesh axis runs over, the one named last changes fastest.
Arguments:
- nodes_zero: float32 [8192, 64], P('row'), may hold values from -28 to 28
- nodes_one: float32 [8192, 64], P(('row', 'col')), may hold values from -28 to 28
- nodes_two: float32 [8192, 64], P('col'), may hold values from -28 to 28
- precision: float32 [64], replicated, may hold values from 0.1 to 0.4
- drift: float32 [64], replicated, may hold values from -1.2 to 1.2
- terminal: bfloat16 [8192, 128], P('col'), may hold values from -6 to 6
- exercise_one: float32 [8192, 128], P(('row', 'col')), may hold values from -6 to 6
- exercise_zero: float32 [8192, 128], P(('row', 'col')), may hold values from -6 to 6
- exercise_flags: int32 [2, 128], replicated, may hold values 0 or 1
Outputs:
- value_one: float32 [8192, 128], P(('row', 'col'))
- value_zero: float32 [8192, 128], P(('row', 'col'))
All inputs are finite; a program needn't handle non-finite values.
Results may differ from a plain program's by a relative error of at most 0.0012.
Values may be sent and summed in bfloat16 or wider, within the bound.
A program may use at most 64 MiB of HBM per device.

v0:
```python
import functools

import jax
import jax.numpy as jnp
from jax import lax
from jax.experimental import pallas as pl
from jax.experimental.pallas import tpu as pltpu
from jax.sharding import PartitionSpec as P

MESH = pl.DeviceIdType.MESH
TILE = 256
PARTS = 2
LIMIT = 62 * 1024 * 1024


def column_of(row):
    return jnp.broadcast_to(row, (128, row.shape[1])).T[:, :1]


def queries_of(nodes, precision, drift, height):
    shifted = nodes + drift
    offsets = 0.5 * jnp.sum(precision * shifted * shifted, axis=0, keepdims=True)
    first = offsets.astype(jnp.bfloat16).astype(jnp.float32)
    rest = offsets - first
    second = rest.astype(jnp.bfloat16).astype(jnp.float32)
    third = rest - second
    count = height - nodes.shape[0]
    at = lax.broadcasted_iota(jnp.int32, (count, nodes.shape[1]), 0)
    extra = jnp.where(at == 0, first, jnp.where(at == 1, second, jnp.where(at == 2, third, 0.0)))
    return jnp.concatenate([shifted * precision, extra], axis=0)


def upright(tall, lanes):
    short = lanes - tall.shape[0]
    if short:
        tall = jnp.concatenate([tall, jnp.zeros((short, tall.shape[1]), tall.dtype)], axis=0)
    return tall.T.astype(jnp.bfloat16)


def ones_under(count, width):
    at = lax.broadcasted_iota(jnp.int32, (count, width), 0)
    return jnp.where(at < 3, -1.0, 0.0).astype(jnp.bfloat16)


def body(
    rows,
    cols,
    nz_hbm,
    n1_hbm,
    n2_hbm,
    precision_hbm,
    drift_hbm,
    terminal_hbm,
    ex1_hbm,
    ex0_hbm,
    flags_hbm,
    v1_hbm,
    v0_hbm,
    precision_ref,
    drift_ref,
    flags_ref,
    nz_ref,
    n1_ref,
    n2_ref,
    terminal_ref,
    ex1_ref,
    ex0_ref,
    v1_ref,
    v0_ref,
    q1t,
    q1,
    t1,
    q0,
    t2,
    e1,
    e0,
    w0,
    st1,
    st0,
    f1,
    f0,
    price,
    out1,
    in1,
    out0,
    in0,
    q_send,
    q_recv,
    t_send,
    t_recv,
    s1_send,
    s1_recv,
    s0_send,
    s0_recv,
    p_send,
    p_recv,
    r1_send,
    r1_recv,
    r0_send,
    r0_recv,
    local,
):
    r = lax.axis_index("row")
    c = lax.axis_index("col")
    depth, own = n1_ref.shape
    sources = nz_ref.shape[1]
    lanes = q0.shape[1]
    height = q1t.shape[1]
    chunks, _, width = e1.shape
    barrier = pltpu.get_barrier_semaphore()
    for d in range(1, rows):
        pl.semaphore_signal(barrier, inc=1, device_id=(lax.rem(r + d, rows), c), device_id_type=MESH)
    for d in range(1, cols):
        pl.semaphore_signal(barrier, inc=1, device_id=(r, lax.rem(c + d, cols)), device_id_type=MESH)

    loads = [
        pltpu.make_async_copy(a, b, local.at[i])
        for i, (a, b) in enumerate(
            [
                (n1_hbm, n1_ref),
                (n2_hbm, n2_ref),
                (nz_hbm, nz_ref),
                (terminal_hbm, terminal_ref),
                (ex1_hbm, ex1_ref),
                (ex0_hbm, ex0_ref),
                (flags_hbm, flags_ref),
                (precision_hbm, precision_ref),
                (drift_hbm, drift_ref),
            ]
        )
    ]
    for load in loads[7:] + loads[:7]:
        load.start()
    loads[7].wait()
    loads[8].wait()
    precision = column_of(precision_ref[...])
    drift = column_of(drift_ref[...])
    loads[0].wait()
    mine = queries_of(n1_ref[...], precision, drift, height)
    q1t[c] = mine.astype(jnp.bfloat16)
    t1[r, :depth, :] = n1_ref[...].astype(jnp.bfloat16)
    for i in range(rows):
        t1[i, depth:, :] = ones_under(lanes - depth, own)
    loads[1].wait()
    for k in range(chunks):
        t2[k, :depth, :] = n2_ref[:, k * width : (k + 1) * width].astype(jnp.bfloat16)
        t2[k, depth:, :] = ones_under(lanes - depth, width)
    q1[c] = upright(mine, lanes)
    pl.semaphore_wait(barrier, rows + cols - 2)

    def to_rows(buf, send, recv):
        def make(d, slot):
            view = buf.at[slot, pl.ds(0, depth)] if buf is t1 else buf.at[slot]
            return pltpu.make_async_remote_copy(
                src_ref=view,
                dst_ref=view,
                send_sem=send.at[d],
                recv_sem=recv.at[d],
                device_id=(lax.rem(r + d, rows), c),
                device_id_type=MESH,
            )

        return make

    def start_rows(buf, send, recv):
        make = to_rows(buf, send, recv)
        for d in range(1, rows):
            make(d, r).start()

    def recv_rows(buf, send, recv):
        make = to_rows(buf, send, recv)
        for d in range(1, rows):
            make(d, lax.rem(r + rows - d, rows)).wait_recv()

    def sent_rows(buf, send, recv):
        make = to_rows(buf, send, recv)
        for d in range(1, rows):
            make(d, r).wait_send()

    def q_copy(d, slot):
        return pltpu.make_async_remote_copy(
            src_ref=q1t.at[slot],
            dst_ref=q1t.at[slot],
            send_sem=q_send.at[d],
            recv_sem=q_recv.at[d],
            device_id=(r, lax.rem(c + d, cols)),
            device_id_type=MESH,
        )

    for d in range(1, cols):
        q_copy(d, c).start()
    start_rows(t1, t_send, t_recv)

    loads[2].wait()
    q0[...] = upright(queries_of(nz_ref[...], precision, drift, height), lanes)
    step = min(TILE, sources)

    def stats(load_queries, load_targets, e, st, begin, end):
        def one(k, carry):
            target = load_targets(k)
            peak = None
            for at in range(0, sources, step):
                s = lax.dot_general(
                    load_queries(at), target, (((1,), (0,)), ((), ())), preferred_element_type=jnp.float32
                )
                e[k, at : at + step, :] = s
                top = jnp.max(s.reshape(step // 8, 8, width), axis=0)
                peak = top if peak is None else jnp.maximum(peak, top)
            peak = jnp.max(peak, axis=0, keepdims=True)
            total = jnp.zeros((8, width), jnp.float32)
            for at in range(0, sources, step):
                x = jnp.exp(e[k, at : at + step, :] - peak)
                e[k, at : at + step, :] = x
                total = total + jnp.sum(x.reshape(step // 8, 8, width), axis=0)
            st[r, 0, pl.ds(k, 1), :] = peak
            st[r, 1, pl.ds(k, 1), :] = jnp.sum(total, axis=0, keepdims=True)
            return carry

        lax.fori_loop(begin, end, one, 0)

    def factor(st, f):
        peak = st[0, 0]
        for i in range(1, rows):
            peak = jnp.maximum(peak, st[i, 0])
        total = jnp.zeros_like(peak)
        for i in range(rows):
            total = total + st[i, 1] * jnp.exp(st[i, 0] - peak)
        f[...] = jnp.exp(st[r, 0] - peak) * (1.0 / total)

    for d in range(1, cols):
        slot = lax.rem(c + cols - d, cols)
        q_copy(d, slot).wait_recv()
        q1[slot] = upright(q1t[slot].astype(jnp.float32), lanes)

    def q1_rows(at):
        return q1[at // own : (at + step) // own].reshape(step, q1.shape[2])

    stats(q1_rows, lambda k: t2[k], e1, st1, 0, chunks)
    start_rows(st1, s1_send, s1_recv)

    recv_rows(t1, t_send, t_recv)
    per = width // own

    def t1_rows(k):
        if per == 1:
            return t1[k]
        return jnp.concatenate([t1[k * per + i] for i in range(per)], axis=1)

    def stats_zero(begin, end):
        stats(lambda at: q0[at : at + step, :], t1_rows, e0, st0, begin, end)

    half = (chunks + 1) // 2
    stats_zero(0, half)

    recv_rows(st1, s1_send, s1_recv)
    factor(st1, f1)

    def partial_of(weights, load_prices, first, count):
        total = jnp.zeros((count, v1_ref.shape[1]), jnp.float32)
        for k in range(chunks):
            total = total + jnp.dot(weights(k, first, count), load_prices(k), preferred_element_type=jnp.float32)
        return total

    def carry_copy(out, into, send, recv, d, h, count):
        return pltpu.make_async_remote_copy(
            src_ref=out.at[d, pl.ds(h * count, count)],
            dst_ref=into.at[d, pl.ds(h * count, count)],
            send_sem=send.at[h * cols + d],
            recv_sem=recv.at[h * cols + d],
            device_id=(r, lax.rem(c + d, cols)),
            device_id_type=MESH,
        )

    def send_carry(weights, load_prices, out, into, send, recv, parts):
        count = own // parts
        for h in range(parts):
            for d in range(1, cols):
                first = lax.rem(c + d, cols) * own + h * count
                part = partial_of(weights, load_prices, first, count)
                out[d, h * count : (h + 1) * count, :] = part.astype(out.dtype)
                carry_copy(out, into, send, recv, d, h, count).start()
        return partial_of(weights, load_prices, c * own, own)

    def take_carry(total, out, into, send, recv, parts, h):
        count = own // parts
        piece = slice(h * count, (h + 1) * count)
        total = total[piece]
        for d in range(1, cols):
            carry_copy(out, into, send, recv, d, h, count).wait_recv()
            total = total + into[d, piece, :].astype(jnp.float32)
        return total

    def end_carry(out, into, send, recv, parts):
        for h in range(parts):
            for d in range(1, cols):
                carry_copy(out, into, send, recv, d, h, own // parts).wait_send()

    def weights_one(k, first, count):
        return (e1[k, pl.ds(first, count), :] * f1[pl.ds(k, 1), :]).astype(jnp.bfloat16)

    loads[3].wait()
    one = (out1, in1, r1_send, r1_recv, PARTS)
    held = send_carry(weights_one, lambda k: terminal_ref[k * width : (k + 1) * width, :], *one)
    stats_zero(half, chunks)
    start_rows(st0, s0_send, s0_recv)
    loads[4].wait()
    loads[6].wait()
    partner = r + 1 - 2 * lax.rem(r, 2)
    half_rows = rows // 2

    size = own // PARTS

    def along(k, h, slot):
        view = price.at[slot, pl.ds(h * size, size)]
        return pltpu.make_async_remote_copy(
            src_ref=view,
            dst_ref=view,
            send_sem=p_send.at[h * rows + k],
            recv_sem=p_recv.at[h * rows + k],
            device_id=(lax.rem(r + 2 * k, rows), c),
            device_id_type=MESH,
        )

    def across(k, h, slot):
        view = price.at[slot, pl.ds(h * size, size)]
        return pltpu.make_async_remote_copy(
            src_ref=view,
            dst_ref=view,
            send_sem=p_send.at[h * rows + half_rows + k],
            recv_sem=p_recv.at[h * rows + half_rows + k],
            device_id=(partner, c),
            device_id_type=MESH,
        )

    for h in range(PARTS):
        piece = slice(h * size, (h + 1) * size)
        carried = take_carry(held, *one, h)
        value = jnp.where(flags_ref[1:2, :] == 1, jnp.maximum(ex1_ref[piece, :], carried), carried)
        v1_ref[piece, :] = value
        price[r, piece, :] = value.astype(jnp.bfloat16)
        for k in range(1, half_rows):
            along(k, h, r).start()
        across(0, h, r).start()
    keep_one = pltpu.make_async_copy(v1_ref, v1_hbm, local.at[9])
    keep_one.start()

    recv_rows(st0, s0_send, s0_recv)
    factor(st0, f0)

    def weigh(k, carry):
        for at in range(0, sources, step):
            w0[k, at : at + step, :] = (e0[k, at : at + step, :] * f0[pl.ds(k, 1), :]).astype(jnp.bfloat16)
        return carry

    lax.fori_loop(0, chunks, weigh, 0)
    for h in range(PARTS):
        for k in range(1, half_rows):
            slot = lax.rem(r + rows - 2 * k, rows)
            along(k, h, slot).wait_recv()
            across(k, h, slot).start()
    for h in range(PARTS):
        for k in range(half_rows):
            across(k, h, lax.rem(partner + rows - 2 * k, rows)).wait_recv()

    def price_rows(k):
        return price[k * per : (k + 1) * per].reshape(width, price.shape[2])

    def weights_zero(k, first, count):
        return w0[k, pl.ds(first, count), :]

    zero = (out0, in0, r0_send, r0_recv, 1)
    held = send_carry(weights_zero, price_rows, *zero)
    loads[5].wait()
    carried = take_carry(held, *zero, 0)
    v0_ref[...] = jnp.where(flags_ref[0:1, :] == 1, jnp.maximum(ex0_ref[...], carried), carried)
    keep_zero = pltpu.make_async_copy(v0_ref, v0_hbm, local.at[10])
    keep_zero.start()

    for d in range(1, cols):
        q_copy(d, c).wait_send()
    sent_rows(t1, t_send, t_recv)
    sent_rows(st1, s1_send, s1_recv)
    sent_rows(st0, s0_send, s0_recv)
    for h in range(PARTS):
        for k in range(half_rows):
            across(k, h, r).wait_send()
            if k:
                along(k, h, r).wait_send()
    end_carry(*one)
    end_carry(*zero)
    keep_one.wait()
    keep_zero.wait()


def shards(rows, cols, nodes_zero, nodes_one, nodes_two, precision, drift, terminal, ex1, ex0, flags):
    own, depth = nodes_one.shape
    height = depth + 16
    sources = nodes_zero.shape[0]
    targets = nodes_two.shape[0]
    trades = terminal.shape[1]
    width = max(own, min(TILE, targets))
    chunks = targets // width
    lanes = 128 * (-(-(depth + 3) // 128))
    dma = pltpu.SemaphoreType.DMA
    out = jax.ShapeDtypeStruct((own, trades), jnp.float32)
    stat = pltpu.VMEM((rows, 2, chunks, width), jnp.float32)
    tall = pltpu.VMEM((chunks, sources, width), jnp.float32)
    few = pltpu.VMEM((chunks, width), jnp.float32)
    parts = pltpu.VMEM((cols, own, trades), jnp.float32)
    slim = pltpu.VMEM((cols, own, trades), jnp.bfloat16)
    anywhere = pl.BlockSpec(memory_space=pl.ANY)
    mine = pltpu.VMEM((own, trades), jnp.float32)
    return pl.pallas_call(
        functools.partial(body, rows, cols),
        out_shape=(out, out),
        in_specs=[pl.BlockSpec(memory_space=pltpu.HBM)] * 9,
        out_specs=(anywhere, anywhere),
        scratch_shapes=[
            pltpu.VMEM((1, depth), jnp.float32),
            pltpu.VMEM((1, depth), jnp.float32),
            pltpu.VMEM((2, trades), jnp.int32),
            pltpu.VMEM((depth, sources), jnp.float32),
            pltpu.VMEM((depth, own), jnp.float32),
            pltpu.VMEM((depth, targets), jnp.float32),
            pltpu.VMEM((targets, trades), jnp.bfloat16),
            mine,
            mine,
            mine,
            mine,
            pltpu.VMEM((cols, height, own), jnp.bfloat16),
            pltpu.VMEM((cols, own, lanes), jnp.bfloat16),
            pltpu.VMEM((rows, lanes, own), jnp.bfloat16),
            pltpu.VMEM((sources, lanes), jnp.bfloat16),
            pltpu.VMEM((chunks, lanes, width), jnp.bfloat16),
            tall,
            tall,
            pltpu.VMEM((chunks, sources, width), jnp.bfloat16),
            stat,
            stat,
            few,
            few,
            pltpu.VMEM((rows, own, trades), jnp.bfloat16),
            parts,
            parts,
            slim,
            slim,
            *[dma((cols,))] * 2,
            *[dma((rows,))] * 6,
            *[dma((PARTS * rows,))] * 2,
            *[dma((PARTS * cols,))] * 2,
            *[dma((cols,))] * 2,
            dma((11,)),
        ],
        compiler_params=pltpu.CompilerParams(
            collective_id=0, has_side_effects=True, vmem_limit_bytes=LIMIT
        ),
    )(nodes_zero.T, nodes_one.T, nodes_two.T, precision[None, :], drift[None, :], terminal, ex1, ex0, flags)


def solution(mesh):
    both = P(("row", "col"), None)
    return jax.shard_map(
        functools.partial(shards, mesh.shape["row"], mesh.shape["col"]),
        mesh=mesh,
        in_specs=(P("row", None), both, P("col", None), P(), P(), P("col", None), both, both, P()),
        out_specs=(both, both),
        check_vma=False,
    )
```

profile of v0, /device:TPU:0, one launch (start us, length us, event | category | flops | bytes accessed | tf_op | source)
XLA Modules:
  0.0 44.0 jit_solution(7195178235496706855)
XLA Ops:
  0.6 41.1 %shard_map.104 = (f32[256,128]{1,0:T(8,128)}, f32[256,128]{1,0:T(8,128)}) custom-call(f32[64,1024]{1,0:T(8,128)} %bitcast.6, f32[64,256]{1,0:T(8,128)} %bitcast.7, f32[64,2048]{1,0:T(8,128)} %bitcast.5, f32[1,64]{1,0:T(1,128)} %bitcast.8, f32[1,64]{1,0:T(1,128)} %bitcast.9, bf16[2048,128]{1,0:T(8,128)(2,1)} %terminal_hbm.1, f32[256,128]{1,0:T(8,128)} %ex1_hbm.1, ...), custom_call_target="tpu_custom_call" | custom-call | tf_op jit(solution)/shard_map/pallas_call | solution.py:413
  41.8 0.0 copy-start
  41.8 1.6 %copy.13 = f32[256,128]{1,0:T(8,128)} copy(f32[256,128]{1,0:T(8,128)} %get-tuple-element.4) | data formatting | bytes 262144
  43.4 0.0 copy-done
  43.4 0.7 %copy.14 = f32[256,128]{1,0:T(8,128)} copy(f32[256,128]{1,0:T(8,128)S(1)} %copy-done) | data formatting | bytes 262144
Async XLA Ops:
  41.8 1.6 %copy-start = (f32[256,128]{1,0:T(8,128)S(1)}, f32[256,128]{1,0:T(8,128)}, u32[]{:S(2)}) copy-start(f32[256,128]{1,0:T(8,128)} %get-tuple-element.5) | copy-start | bytes 393220
where the time goes:
time: 44.2 us; the launch traced here: 44 us
  Pallas kernels  41.1 us (93%)
  local copies, waits for them, and re-layouts  2.26 us (5%)
  between operations  0.65 us (1%)
    pallas_call x1, Pallas kernels, shards(): pl.pallas_call(functools.partial(body, rows, cols), out_shape=(out, out),...  41.1 us
    unnamed x4, local copies, waits for them, and re-layouts  2.26 us

commit v1 on v0

--- a/solution.py
+++ b/solution.py
@@ -10,7 +10,7 @@
 MESH = pl.DeviceIdType.MESH
 TILE = 256
 PARTS = 2
-LIMIT = 62 * 1024 * 1024
+LIMIT = 60 * 1024 * 1024
 
 
 def column_of(row):
@@ -341,8 +341,7 @@
         for k in range(1, half_rows):
             along(k, h, r).start()
         across(0, h, r).start()
-    keep_one = pltpu.make_async_copy(v1_ref, v1_hbm, local.at[9])
-    keep_one.start()
+    v1_hbm[...] = v1_ref[...]
 
     recv_rows(st0, s0_send, s0_recv)
     factor(st0, f0)
@@ -373,8 +372,7 @@
     loads[5].wait()
     carried = take_carry(held, *zero, 0)
     v0_ref[...] = jnp.where(flags_ref[0:1, :] == 1, jnp.maximum(ex0_ref[...], carried), carried)
-    keep_zero = pltpu.make_async_copy(v0_ref, v0_hbm, local.at[10])
-    keep_zero.start()
+    v0_hbm[...] = v0_ref[...]
 
     for d in range(1, cols):
         q_copy(d, c).wait_send()
@@ -388,8 +386,6 @@
                 along(k, h, r).wait_send()
     end_carry(*one)
     end_carry(*zero)
-    keep_one.wait()
-    keep_zero.wait()
 
 
 def shards(rows, cols, nodes_zero, nodes_one, nodes_two, precision, drift, terminal, ex1, ex0, flags):
@@ -408,11 +404,11 @@
     few = pltpu.VMEM((chunks, width), jnp.float32)
     parts = pltpu.VMEM((cols, own, trades), jnp.float32)
     slim = pltpu.VMEM((cols, own, trades), jnp.bfloat16)
-    anywhere = pl.BlockSpec(memory_space=pl.ANY)
+    anywhere = pl.BlockSpec(memory_space=pltpu.VMEM)
     mine = pltpu.VMEM((own, trades), jnp.float32)
-    return pl.pallas_call(
+    one, zero = pl.pallas_call(
         functools.partial(body, rows, cols),
-        out_shape=(out, out),
+        out_shape=(pltpu.VMEM((own, trades), jnp.float32),) * 2,
         in_specs=[pl.BlockSpec(memory_space=pltpu.HBM)] * 9,
         out_specs=(anywhere, anywhere),
         scratch_shapes=[
@@ -455,6 +451,28 @@
             collective_id=0, has_side_effects=True, vmem_limit_bytes=LIMIT
         ),
     )(nodes_zero.T, nodes_one.T, nodes_two.T, precision[None, :], drift[None, :], terminal, ex1, ex0, flags)
+    return handed(one, zero)
+
+
+def hand(a, b, c, d, sems):
+    copies = [pltpu.make_async_copy(a, c, sems.at[0]), pltpu.make_async_copy(b, d, sems.at[1])]
+    for copy in copies:
+        copy.start()
+    for copy in copies:
+        copy.wait()
+
+
+def handed(one, zero):
+    here = pl.BlockSpec(memory_space=pltpu.VMEM)
+    out = jax.ShapeDtypeStruct(one.shape, one.dtype)
+    return pl.pallas_call(
+        hand,
+        out_shape=(out, out),
+        in_specs=[here, here],
+        out_specs=(pl.BlockSpec(memory_space=pltpu.HBM),) * 2,
+        scratch_shapes=[pltpu.SemaphoreType.DMA((2,))],
+        compiler_params=pltpu.CompilerParams(vmem_limit_bytes=2 * 1024 * 1024),
+    )(one, zero)
 
 
 def solution(mesh):

time: 44.2 us -> 42.1 us (0.952)
  local copies, waits for them, and re-layouts: 2.26 us -> 0 us
    unnamed x4 -> x0, local copies, waits for them, and re-layouts: 2.26 us -> none
    pallas_call x1 -> x2, Pallas kernels: 41.1 us -> 41.3 us  [the longest x1 40.6 us: shards(): pl.pallas_call(functools.partial(body, rows, cols), out_shape=(pltpu.VMEM...]
where the time goes in v1:
time: 42.1 us; the launch traced here: 42 us
  Pallas kernels  41.3 us (98%)
  between operations  0.64 us (2%)
    pallas_call x1, Pallas kernels, shards(): pl.pallas_call(functools.partial(body, rows, cols), out_shape=(pltpu.VMEM...  40.6 us

profile of v1, /device:TPU:0, one launch (start us, length us, event | category | flops | bytes accessed | tf_op | source)
XLA Modules:
  0.0 42.0 jit_solution(3479944385359534580)
XLA Ops:
  0.6 40.6 %shard_map.104 = (f32[256,128]{1,0:T(8,128)S(1)}, f32[256,128]{1,0:T(8,128)S(1)}) custom-call(f32[64,1024]{1,0:T(8,128)} %bitcast.6, f32[64,256]{1,0:T(8,128)} %bitcast.7, f32[64,2048]{1,0:T(8,128)} %bitcast.5, f32[1,64]{1,0:T(1,128)} %bitcast.8, f32[1,64]{1,0:T(1,128)} %bitcast.9, bf16[2048,128]{1,0:T(8,128)(2,1)} %terminal_hbm.1, f32[256,128]{1,0:T(8,128)} %ex1_hbm.1, ...), custom_call_target="tpu_custom_call" | custom-call | tf_op jit(solution)/shard_map/pallas_call | solution.py:409
  41.2 0.7 %shard_map.105 = (f32[256,128]{1,0:T(8,128)}, f32[256,128]{1,0:T(8,128)}) custom-call(f32[256,128]{1,0:T(8,128)S(1)} %get-tuple-element.4.a, f32[256,128]{1,0:T(8,128)S(1)} %get-tuple-element.5.b), custom_call_target="tpu_custom_call" | custom-call | tf_op jit(solution)/shard_map/pallas_call | solution.py:468

commit v2 on v1

v2 whole, which is shorter than its diff:
```python
import functools

import jax
import jax.numpy as jnp
from jax import lax
from jax.experimental import pallas as pl
from jax.experimental.pallas import tpu as pltpu
from jax.sharding import PartitionSpec as P

MESH = pl.DeviceIdType.MESH
TILE = 256
PARTS = 2
LAST = 2
LIMIT = 60 * 1024 * 1024


def flip(index, mask, size):
    bit = 1
    while bit < size:
        if mask & bit:
            index = index + bit - 2 * bit * lax.rem(lax.div(index, bit), 2)
        bit *= 2
    return index


def column_of(row):
    return jnp.broadcast_to(row, (128, row.shape[1])).T[:, :1]


def queries_of(nodes, precision, drift, height):
    shifted = nodes + drift
    offsets = 0.5 * jnp.sum(precision * shifted * shifted, axis=0, keepdims=True)
    first = offsets.astype(jnp.bfloat16).astype(jnp.float32)
    rest = offsets - first
    second = rest.astype(jnp.bfloat16).astype(jnp.float32)
    third = rest - second
    count = height - nodes.shape[0]
    at = lax.broadcasted_iota(jnp.int32, (count, nodes.shape[1]), 0)
    extra = jnp.where(at == 0, first, jnp.where(at == 1, second, jnp.where(at == 2, third, 0.0)))
    return jnp.concatenate([shifted * precision, extra], axis=0)


def upright(tall, lanes):
    short = lanes - tall.shape[0]
    if short:
        tall = jnp.concatenate([tall, jnp.zeros((short, tall.shape[1]), tall.dtype)], axis=0)
    return tall.T.astype(jnp.bfloat16)


def ones_under(count, width):
    at = lax.broadcasted_iota(jnp.int32, (count, width), 0)
    return jnp.where(at < 3, -1.0, 0.0).astype(jnp.bfloat16)


def settled(allowed, exercise, carried):
    return jnp.where(allowed == 1, jnp.maximum(exercise, carried), carried)


def scored(queries, targets):
    s = lax.dot_general(queries, targets, (((1,), (0,)), ((), ())), preferred_element_type=jnp.float32)
    fold = (s.shape[0] // 8, 8, s.shape[1])
    peak = jnp.max(jnp.max(s.reshape(fold), axis=0), axis=0, keepdims=True)
    x = jnp.exp(s - peak)
    return x, peak, jnp.sum(jnp.sum(x.reshape(fold), axis=0), axis=0, keepdims=True)


def merged(levels, totals):
    top = functools.reduce(jnp.maximum, levels)
    total = None
    for i, level in enumerate(levels):
        term = jnp.exp(level - top)
        if totals is not None:
            term = totals[i] * term
        total = term if total is None else total + term
    return top + jnp.log(total)


def body(
    rows,
    cols,
    nz_hbm,
    n1_hbm,
    n2_hbm,
    precision_hbm,
    drift_hbm,
    terminal_hbm,
    ex1_hbm,
    ex0_hbm,
    flags_hbm,
    v1_ref,
    v0_ref,
    precision_ref,
    drift_ref,
    flags_ref,
    nz_ref,
    n1_ref,
    n2_ref,
    terminal_ref,
    ex1_ref,
    ex0_ref,
    q1t,
    q1,
    t1,
    q0a,
    q0,
    t2,
    e1,
    e0,
    pk1,
    tt1,
    f1,
    pk0,
    tt0,
    f0,
    l1,
    l0,
    price,
    acc1,
    acc0,
    pair_out1,
    pair_in1,
    far_out1,
    far_in1,
    pair_out0,
    pair_in0,
    far_out0,
    far_in0,
    q_send,
    q_recv,
    t_send,
    t_recv,
    l1_send,
    l1_recv,
    l0_send,
    l0_recv,
    p_send,
    p_recv,
    pair1_send,
    pair1_recv,
    far1_send,
    far1_recv,
    pair0_send,
    pair0_recv,
    far0_send,
    far0_recv,
    local,
):
    r = lax.axis_index("row")
    c = lax.axis_index("col")
    depth, own = n1_ref.shape
    lanes = q0.shape[1]
    height = q1t.shape[1]
    _, chunks, _, width = e1.shape
    trades = price.shape[2]
    sources = q0.shape[0]
    blocks, _, _ = pk0.shape
    step = sources // blocks
    halves = l1.shape[1]
    some = chunks // halves

    def row_peer(m):
        return (flip(r, m, rows), c)

    def col_peer(s):
        return (r, flip(c, s, cols))

    def remote(src, dst, send, recv, peer):
        return pltpu.make_async_remote_copy(
            src_ref=src, dst_ref=dst, send_sem=send, recv_sem=recv, device_id=peer, device_id_type=MESH
        )

    barrier = pltpu.get_barrier_semaphore()
    for m in range(1, rows):
        pl.semaphore_signal(barrier, inc=1, device_id=row_peer(m), device_id_type=MESH)
    for s in range(1, cols):
        pl.semaphore_signal(barrier, inc=1, device_id=col_peer(s), device_id_type=MESH)
    loads = [
        pltpu.make_async_copy(a, b, local.at[i])
        for i, (a, b) in enumerate(
            [
                (precision_hbm, precision_ref),
                (drift_hbm, drift_ref),
                (n1_hbm, n1_ref),
                (n2_hbm, n2_ref),
                (nz_hbm, nz_ref),
                (terminal_hbm, terminal_ref),
                (ex1_hbm, ex1_ref),
                (flags_hbm, flags_ref),
                (ex0_hbm, ex0_ref),
            ]
        )
    ]
    for load in loads:
        load.start()
    for load in loads[:3]:
        load.wait()
    precision = column_of(precision_ref[...])
    drift = column_of(drift_ref[...])
    mine = queries_of(n1_ref[...], precision, drift, height)
    q1t[0] = mine.astype(jnp.bfloat16)
    t1[0, :depth, :] = n1_ref[...].astype(jnp.bfloat16)
    pl.semaphore_wait(barrier, rows + cols - 2)

    def q_copy(s):
        return remote(q1t.at[0], q1t.at[s], q_send.at[s], q_recv.at[s], col_peer(s))

    far_first = list(range(2, cols, 2)) + list(range(3, cols, 2)) + [1]
    for s in far_first:
        q_copy(s).start()

    def t_copy(m):
        if m % 2:
            src, peer = t1.at[m - 1, pl.ds(0, depth)], row_peer(1)
        else:
            src, peer = t1.at[0, pl.ds(0, depth)], row_peer(m)
        return remote(src, t1.at[m, pl.ds(0, depth)], t_send.at[m], t_recv.at[m], peer)

    for m in range(2, rows, 2):
        t_copy(m).start()
    t_copy(1).start()

    q1[0] = upright(mine, lanes)
    for m in range(rows):
        t1[m, depth:, :] = ones_under(lanes - depth, own)
    loads[3].wait()
    for k in range(chunks):
        t2[k, :depth, :] = n2_ref[:, k * width : (k + 1) * width].astype(jnp.bfloat16)
        t2[k, depth:, :] = ones_under(lanes - depth, width)

    def stats_one(s, first, last):
        for k in range(first, last):
            x, peak, total = scored(q1[s], t2[k])
            e1[s, k] = x
            pk1[s, k : k + 1, :] = peak
            tt1[s, k : k + 1, :] = total

    def stats_zero(m):
        row = flip(r, m, rows)
        for b in range(blocks):
            x, peak, total = scored(q0[b * step : (b + 1) * step, :], t1[m])
            e0[m, b * step : (b + 1) * step, :] = x
            pk0[b, pl.ds(row, 1), :] = peak
            tt0[b, pl.ds(row, 1), :] = total

    def take_q(s):
        q_copy(s).wait_recv()
        q1[s] = upright(q1t[s].astype(jnp.float32), lanes)

    stats_one(0, 0, chunks)
    take_q(1)
    stats_one(1, 0, chunks)
    loads[4].wait()
    q0a[...] = upright(queries_of(nz_ref[...], precision, drift, height), lanes)
    for s in range(cols):
        q0[s * own : (s + 1) * own, :] = q0a[pl.ds(pl.multiple_of(flip(c, s, cols) * own, own), own), :]
    stats_zero(0)
    for s in far_first[:-2]:
        take_q(s)
        stats_one(s, 0, chunks)

    def l1_copy(m, h):
        at = h * rows + m
        return remote(l1.at[0, h], l1.at[m, h], l1_send.at[at], l1_recv.at[at], row_peer(m))

    final = far_first[-2] if cols > 2 else None
    if final is not None:
        take_q(final)
    for h in range(halves):
        part = slice(h * some, (h + 1) * some)
        if final is not None:
            stats_one(final, h * some, (h + 1) * some)
        l1[0, h] = merged([pk1[s, part, :] for s in range(cols)], [tt1[s, part, :] for s in range(cols)])
        for m in range(1, rows):
            l1_copy(m, h).start()

    for m in range(2, rows, 2):
        t_copy(m).wait_recv()
        t_copy(m + 1).start()
    for m in range(2, rows, 2):
        stats_zero(m)
    t_copy(1).wait_recv()
    stats_zero(1)

    def weights_one(s, k):
        return (e1[s, k] * f1[s, k : k + 1, :]).astype(jnp.bfloat16)

    def partial_one(s, total, first, last):
        for k in range(first, last):
            part = jnp.dot(
                weights_one(s, k), terminal_ref[k * width : (k + 1) * width, :], preferred_element_type=jnp.float32
            )
            total = part if total is None else total + part
        return total

    def pair_copy(out, into, send, recv, s):
        return remote(out.at[s // 2], into.at[s // 2], send.at[s // 2], recv.at[s // 2], col_peer(1))

    def far_copy(out, into, send, recv, s, h, count):
        at = h * (cols // 2) + s // 2
        piece = pl.ds(h * count, count)
        return remote(out.at[s // 2, piece], into.at[s // 2, piece], send.at[at], recv.at[at], col_peer(s))

    pair1 = (pair_out1, pair_in1, pair1_send, pair1_recv)
    far1 = (far_out1, far_in1, far1_send, far1_recv)
    pair0 = (pair_out0, pair_in0, pair0_send, pair0_recv)
    far0 = (far_out0, far_in0, far0_send, far0_recv)
    size = own // PARTS
    away = list(range(2, cols, 2))

    for h in range(halves):
        part = slice(h * some, (h + 1) * some)
        for m in range(1, rows):
            l1_copy(m, h).wait_recv()
        if h == 0:
            loads[5].wait()
        level = merged([l1[m, h] for m in range(rows)], None)
        for s in range(cols):
            f1[s, part, :] = jnp.exp(pk1[s, part, :] - level)
        last = h == halves - 1
        for s in [s + 1 for s in away] + [1] + away + [0]:
            total = partial_one(s, acc1[s] if h else None, h * some, (h + 1) * some)
            if last and s % 2:
                pair_out1[s // 2] = total
                pair_copy(*pair1, s - 1).start()
            else:
                acc1[s] = total
    for s in away:
        pair_copy(*pair1, s).wait_recv()
        for h in range(PARTS):
            piece = slice(h * size, (h + 1) * size)
            far_out1[s // 2, piece, :] = acc1[s, piece, :] + pair_in1[s // 2, piece, :]
            far_copy(*far1, s, h, size).start()
    pair_copy(*pair1, 0).wait_recv()
    held = acc1[0] + pair_in1[0]

    for m in range(3, rows, 2):
        t_copy(m).wait_recv()
        stats_zero(m)
    l0[0] = merged([pk0[b] for b in range(blocks)], [tt0[b] for b in range(blocks)])

    def l0_copy(m):
        return remote(l0.at[0], l0.at[m], l0_send.at[m], l0_recv.at[m], row_peer(m))

    for m in range(1, rows):
        l0_copy(m).start()
    loads[6].wait()
    loads[7].wait()

    def p_copy(m, h):
        piece = pl.ds(h * size, size)
        at = h * rows + m
        if m % 2:
            src, peer = price.at[m - 1, piece], row_peer(1)
        else:
            src, peer = price.at[0, piece], row_peer(m)
        return remote(src, price.at[m, piece], p_send.at[at], p_recv.at[at], peer)

    for h in range(PARTS):
        piece = slice(h * size, (h + 1) * size)
        carried = held[piece]
        for s in away:
            far_copy(*far1, s, h, size).wait_recv()
            carried = carried + far_in1[s // 2, piece, :]
        value = settled(flags_ref[1:2, :], ex1_ref[piece, :], carried)
        price[0, piece, :] = value.astype(jnp.bfloat16)
        v1_ref[piece, :] = value
        for m in range(2, rows, 2):
            p_copy(m, h).start()
        p_copy(1, h).start()

    for m in range(1, rows):
        l0_copy(m).wait_recv()
    level = merged([l0[m] for m in range(rows)], None)
    for b in range(blocks):
        f0[b] = jnp.exp(pk0[b] - level)

    def add_zero(m, first, count):
        row = flip(r, m, rows)
        parts = []
        each = min(step, count)
        for at in range(first, first + count, each):
            w = (e0[m, at : at + each, :] * f0[at // step, pl.ds(row, 1), :]).astype(jnp.bfloat16)
            parts.append(jnp.dot(w, price[m], preferred_element_type=jnp.float32))
        return parts[0] if len(parts) == 1 else jnp.concatenate(parts, axis=0)

    def gain(m):
        for at in range(0, sources, step):
            part = add_zero(m, at, step)
            acc0[at : at + step, :] = part if m == 0 else acc0[at : at + step, :] + part

    gain(0)
    for h in range(PARTS):
        for m in range(2, rows, 2):
            p_copy(m, h).wait_recv()
            p_copy(m + 1, h).start()
    for m in range(2, rows, 2):
        gain(m)
    for m in range(1, rows - 2, 2):
        for h in range(PARTS):
            p_copy(m, h).wait_recv()
        gain(m)
    for h in range(PARTS):
        p_copy(rows - 1, h).wait_recv()
    count = own // LAST
    for s in [s + 1 for s in away] + [1] + away + [0]:
        total = acc0[s * own : (s + 1) * own, :] + add_zero(rows - 1, s * own, own)
        if s % 2:
            pair_out0[s // 2] = total
            pair_copy(*pair0, s - 1).start()
        else:
            acc0[s * own : (s + 1) * own, :] = total
    for s in away:
        pair_copy(*pair0, s).wait_recv()
        for h in range(LAST):
            piece = slice(h * count, (h + 1) * count)
            total = acc0[s * own + h * count : s * own + (h + 1) * count, :] + pair_in0[s // 2, piece, :]
            far_out0[s // 2, piece, :] = total.astype(far_out0.dtype)
            far_copy(*far0, s, h, count).start()
    pair_copy(*pair0, 0).wait_recv()
    held = acc0[:own, :] + pair_in0[0]
    loads[8].wait()
    for h in range(LAST):
        piece = slice(h * count, (h + 1) * count)
        carried = held[piece]
        for s in away:
            far_copy(*far0, s, h, count).wait_recv()
            carried = carried + far_in0[s // 2, piece, :].astype(jnp.float32)
        v0_ref[piece, :] = settled(flags_ref[0:1, :], ex0_ref[piece, :], carried)

    for s in range(1, cols):
        q_copy(s).wait_send()
    for m in range(1, rows):
        t_copy(m).wait_send()
        l0_copy(m).wait_send()
        for h in range(halves):
            l1_copy(m, h).wait_send()
        for h in range(PARTS):
            p_copy(m, h).wait_send()
    for s in range(0, cols, 2):
        pair_copy(*pair1, s).wait_send()
        pair_copy(*pair0, s).wait_send()
    for s in away:
        for h in range(PARTS):
            far_copy(*far1, s, h, size).wait_send()
        for h in range(LAST):
            far_copy(*far0, s, h, count).wait_send()


def shards(rows, cols, nodes_zero, nodes_one, nodes_two, precision, drift, terminal, ex1, ex0, flags):
    own, depth = nodes_one.shape
    height = depth + 16
    sources = nodes_zero.shape[0]
    targets = nodes_two.shape[0]
    trades = terminal.shape[1]
    width = min(TILE, targets)
    chunks = targets // width
    halves = 2 if chunks % 2 == 0 else 1
    step = max(own, min(TILE, sources))
    blocks = sources // step
    lanes = 128 * (-(-(depth + 3) // 128))
    dma = pltpu.SemaphoreType.DMA
    f32, bf16 = jnp.float32, jnp.bfloat16
    row_stat = pltpu.VMEM((cols, chunks, width), f32)
    col_stat = pltpu.VMEM((blocks, rows, own), f32)
    piece = pltpu.VMEM((cols // 2, own, trades), f32)
    slim = pltpu.VMEM((cols // 2, own, trades), bf16)
    mine = pltpu.VMEM((own, trades), f32)
    one, zero = pl.pallas_call(
        functools.partial(body, rows, cols),
        out_shape=(pltpu.VMEM((own, trades), f32),) * 2,
        in_specs=[pl.BlockSpec(memory_space=pltpu.HBM)] * 9,
        out_specs=(pl.BlockSpec(memory_space=pltpu.VMEM),) * 2,
        scratch_shapes=[
            pltpu.VMEM((1, depth), f32),
            pltpu.VMEM((1, depth), f32),
            pltpu.VMEM((2, trades), jnp.int32),
            pltpu.VMEM((depth, sources), f32),
            pltpu.VMEM((depth, own), f32),
            pltpu.VMEM((depth, targets), f32),
            pltpu.VMEM((targets, trades), bf16),
            mine,
            mine,
            pltpu.VMEM((cols, height, own), bf16),
            pltpu.VMEM((cols, own, lanes), bf16),
            pltpu.VMEM((rows, lanes, own), bf16),
            pltpu.VMEM((sources, lanes), bf16),
            pltpu.VMEM((sources, lanes), bf16),
            pltpu.VMEM((chunks, lanes, width), bf16),
            pltpu.VMEM((cols, chunks, own, width), f32),
            pltpu.VMEM((rows, sources, own), f32),
            row_stat,
            row_stat,
            row_stat,
            col_stat,
            col_stat,
            col_stat,
            pltpu.VMEM((rows, halves, chunks // halves, width), f32),
            pltpu.VMEM((rows, rows, own), f32),
            pltpu.VMEM((rows, own, trades), bf16),
            pltpu.VMEM((cols, own, trades), f32),
            pltpu.VMEM((sources, trades), f32),
            *[piece] * 6,
            *[slim] * 2,
            *[dma((cols,))] * 2,
            *[dma((rows,))] * 2,
            *[dma((halves * rows,))] * 2,
            *[dma((rows,))] * 2,
            *[dma((PARTS * rows,))] * 2,
            *[dma((cols // 2,))] * 2,
            *[dma((PARTS * (cols // 2),))] * 2,
            *[dma((cols // 2,))] * 2,
            *[dma((LAST * (cols // 2),))] * 2,
            dma((9,)),
        ],
        compiler_params=pltpu.CompilerParams(
            collective_id=0, has_side_effects=True, vmem_limit_bytes=LIMIT
        ),
    )(nodes_zero.T, nodes_one.T, nodes_two.T, precision[None, :], drift[None, :], terminal, ex1, ex0, flags)
    return handed(one, zero)


def hand(a, b, c, d, sems):
    copies = [pltpu.make_async_copy(a, c, sems.at[0]), pltpu.make_async_copy(b, d, sems.at[1])]
    for copy in copies:
        copy.start()
    for copy in copies:
        copy.wait()


def handed(one, zero):
    here = pl.BlockSpec(memory_space=pltpu.VMEM)
    out = jax.ShapeDtypeStruct(one.shape, one.dtype)
    return pl.pallas_call(
        hand,
        out_shape=(out, out),
        in_specs=[here, here],
        out_specs=(pl.BlockSpec(memory_space=pltpu.HBM),) * 2,
        scratch_shapes=[pltpu.SemaphoreType.DMA((2,))],
        compiler_params=pltpu.CompilerParams(vmem_limit_bytes=2 * 1024 * 1024),
    )(one, zero)


def solution(mesh):
    both = P(("row", "col"), None)
    return jax.shard_map(
        functools.partial(shards, mesh.shape["row"], mesh.shape["col"]),
        mesh=mesh,
        in_specs=(P("row", None), both, P("col", None), P(), P(), P("col", None), both, both, P()),
        out_specs=(both, both),
        check_vma=False,
    )
```

time: 42.1 us -> 37.8 us (0.90)
  Pallas kernels: 41.3 us -> 37 us
    pallas_call x1, Pallas kernels: 40.6 us -> 36.3 us  [shards(): pl.pallas_call(functools.partial(body, rows, cols), out_shape=(pltpu.VMEM...]
where the time goes in v2:
time: 37.8 us; the launch traced here: 37.7 us
  Pallas kernels  37 us (98%)
  between operations  0.64 us (2%)
    pallas_call x1, Pallas kernels, shards(): pl.pallas_call(functools.partial(body, rows, cols), out_shape=(pltpu.VMEM...  36.3 us

profile of v2, /device:TPU:0, one launch (start us, length us, event | category | flops | bytes accessed | tf_op | source)
XLA Modules:
  0.0 37.7 jit_solution(8270062145588189487)
XLA Ops:
  0.6 36.3 %shard_map.104 = (f32[256,128]{1,0:T(8,128)S(1)}, f32[256,128]{1,0:T(8,128)S(1)}) custom-call(f32[64,1024]{1,0:T(8,128)} %bitcast.6, f32[64,256]{1,0:T(8,128)} %bitcast.7, f32[64,2048]{1,0:T(8,128)} %bitcast.5, f32[1,64]{1,0:T(1,128)} %bitcast.8, f32[1,64]{1,0:T(1,128)} %bitcast.9, bf16[2048,128]{1,0:T(8,128)(2,1)} %terminal_hbm.1, f32[256,128]{1,0:T(8,128)} %ex1_hbm.1, ...), custom_call_target="tpu_custom_call" | custom-call | tf_op jit(solution)/shard_map/pallas_call | solution.py:468
  36.9 0.7 %shard_map.105 = (f32[256,128]{1,0:T(8,128)}, f32[256,128]{1,0:T(8,128)}) custom-call(f32[256,128]{1,0:T(8,128)S(1)} %get-tuple-element.4.a, f32[256,128]{1,0:T(8,128)S(1)} %get-tuple-element.5.b), custom_call_target="tpu_custom_call" | custom-call | tf_op jit(solution)/shard_map/pallas_call | solution.py:533

commit v3 on v2

v3 whole, which is shorter than its diff:
```python
import functools

import jax
import jax.numpy as jnp
from jax import lax
from jax.experimental import pallas as pl
from jax.experimental.pallas import tpu as pltpu
from jax.sharding import PartitionSpec as P

MESH = pl.DeviceIdType.MESH
TILE = 256
PARTS = 2
RELAY = 1
LAST = 2
LIMIT = 60 * 1024 * 1024


def flip(index, mask, size):
    bit = 1
    while bit < size:
        if mask & bit:
            index = index + bit - 2 * bit * lax.rem(lax.div(index, bit), 2)
        bit *= 2
    return index


def column_of(row):
    return jnp.broadcast_to(row, (128, row.shape[1])).T[:, :1]


def queries_of(nodes, precision, drift, height):
    shifted = nodes + drift
    offsets = 0.5 * jnp.sum(precision * shifted * shifted, axis=0, keepdims=True)
    first = offsets.astype(jnp.bfloat16).astype(jnp.float32)
    rest = offsets - first
    second = rest.astype(jnp.bfloat16).astype(jnp.float32)
    third = rest - second
    count = height - nodes.shape[0]
    at = lax.broadcasted_iota(jnp.int32, (count, nodes.shape[1]), 0)
    extra = jnp.where(at == 0, first, jnp.where(at == 1, second, jnp.where(at == 2, third, 0.0)))
    return jnp.concatenate([shifted * precision, extra], axis=0)


def upright(tall, lanes):
    short = lanes - tall.shape[0]
    if short:
        tall = jnp.concatenate([tall, jnp.zeros((short, tall.shape[1]), tall.dtype)], axis=0)
    return tall.T.astype(jnp.bfloat16)


def ones_under(count, width):
    at = lax.broadcasted_iota(jnp.int32, (count, width), 0)
    return jnp.where(at < 3, -1.0, 0.0).astype(jnp.bfloat16)


def settled(allowed, exercise, carried):
    return jnp.where(allowed == 1, jnp.maximum(exercise, carried), carried)


def scored(queries, targets):
    s = lax.dot_general(queries, targets, (((1,), (0,)), ((), ())), preferred_element_type=jnp.float32)
    fold = (s.shape[0] // 8, 8, s.shape[1])
    peak = jnp.max(jnp.max(s.reshape(fold), axis=0), axis=0, keepdims=True)
    x = jnp.exp(s - peak)
    return x, peak, jnp.sum(jnp.sum(x.reshape(fold), axis=0), axis=0, keepdims=True)


def merged(levels, totals):
    top = functools.reduce(jnp.maximum, levels)
    total = None
    for i, level in enumerate(levels):
        term = jnp.exp(level - top)
        if totals is not None:
            term = totals[i] * term
        total = term if total is None else total + term
    return top + jnp.log(total)


def body(
    rows,
    cols,
    nz_hbm,
    n1_hbm,
    n2_hbm,
    precision_hbm,
    drift_hbm,
    terminal_hbm,
    ex1_hbm,
    ex0_hbm,
    flags_hbm,
    v1_out,
    v0_out,
    precision_ref,
    drift_ref,
    flags_ref,
    nz_ref,
    n1_ref,
    n2_ref,
    terminal_ref,
    ex1_ref,
    ex0_ref,
    v1_ref,
    v0_ref,
    q1t,
    q1,
    t1,
    q0a,
    q0,
    t2,
    e1,
    e0,
    pk1,
    tt1,
    f1,
    pk0,
    tt0,
    f0,
    l1,
    l0,
    price,
    acc1,
    acc0,
    pair_out1,
    pair_in1,
    far_out1,
    far_in1,
    far_out0,
    far_in0,
    q_send,
    q_recv,
    t_send,
    t_recv,
    l1_send,
    l1_recv,
    l0_send,
    l0_recv,
    p_send,
    p_recv,
    pc_recv,
    pair1_send,
    pair1_recv,
    far1_send,
    far1_recv,
    y_send,
    y_recv,
    far0_send,
    far0_recv,
    local,
    ready,
):
    r = lax.axis_index("row")
    c = lax.axis_index("col")
    depth, own = n1_ref.shape
    lanes = q0.shape[1]
    height = q1t.shape[1]
    _, chunks, _, width = e1.shape
    trades = price.shape[2]
    sources = q0.shape[0]
    blocks, _, _ = pk0.shape
    step = sources // blocks
    near = sources // 2
    group = 2 * lax.div(r, 2) + lax.rem(c, 2)

    def row_peer(m):
        return (flip(r, m, rows), c)

    def col_peer(s):
        return (r, flip(c, s, cols))

    def line_peer(m):
        return (flip(r, m - m % 2, rows), flip(c, m % 2, cols))

    def plane_peer(s):
        return (flip(r, s % 2, rows), flip(c, s - s % 2, cols))

    def remote(src, dst, send, recv, peer):
        return pltpu.make_async_remote_copy(
            src_ref=src, dst_ref=dst, send_sem=send, recv_sem=recv, device_id=peer, device_id_type=MESH
        )

    beside = [col_peer(s) for s in range(1, cols)]
    m = 1
    while m < rows:
        beside.append(row_peer(m))
        m *= 2
    barrier = pltpu.get_barrier_semaphore()

    def call(sem):
        for peer in beside:
            pl.semaphore_signal(sem, inc=1, device_id=peer, device_id_type=MESH)

    call(barrier)
    loads = [
        pltpu.make_async_copy(a, b, local.at[i])
        for i, (a, b) in enumerate(
            [
                (n1_hbm, n1_ref),
                (precision_hbm, precision_ref),
                (drift_hbm, drift_ref),
                (n2_hbm, n2_ref),
                (nz_hbm, nz_ref),
                (terminal_hbm, terminal_ref),
                (ex1_hbm, ex1_ref),
                (flags_hbm, flags_ref),
                (ex0_hbm, ex0_ref),
            ]
        )
    ]
    for load in loads:
        load.start()
    for load in loads[:3]:
        load.wait()
    precision = column_of(precision_ref[...])
    drift = column_of(drift_ref[...])
    mine = queries_of(n1_ref[...], precision, drift, height)
    q1t[0] = mine.astype(jnp.bfloat16)
    t1[0, :depth, :] = n1_ref[...].astype(jnp.bfloat16)
    pl.semaphore_wait(barrier, len(beside))
    call(ready.at[0])

    def q_copy(s):
        return remote(q1t.at[0], q1t.at[s], q_send.at[0], q_recv.at[s - 1], col_peer(s))

    far = list(range(2, cols, 2)) + list(range(3, cols, 2))
    for s in [1] + far:
        q_copy(s).start()

    def t_copy(m):
        if m % 2:
            src, peer = t1.at[m - 1, pl.ds(0, depth)], col_peer(1)
        else:
            src, peer = t1.at[0, pl.ds(0, depth)], row_peer(m)
        return remote(src, t1.at[m, pl.ds(0, depth)], t_send.at[0], t_recv.at[m % 2], peer)

    t_copy(1).start()
    soon = [m for m in range(2, rows, 2) if m & (m - 1) == 0]
    late = [m for m in range(2, rows, 2) if m & (m - 1)]
    for m in soon:
        t_copy(m).start()

    q1[0] = upright(mine, lanes)
    for m in range(rows):
        t1[m, depth:, :] = ones_under(lanes - depth, own)
    loads[3].wait()
    for k in range(chunks):
        t2[k, :depth, :] = n2_ref[:, k * width : (k + 1) * width].astype(jnp.bfloat16)
        t2[k, depth:, :] = ones_under(lanes - depth, width)

    def stats_one(s):
        for k in range(chunks):
            x, peak, total = scored(q1[s], t2[k])
            e1[s, k] = x
            pk1[s, k : k + 1, :] = peak
            tt1[s, k : k + 1, :] = total

    def stats_zero(m, first, last):
        row = flip(group, m, rows)
        for b in range(first, last):
            x, peak, total = scored(q0[b * step : (b + 1) * step, :], t1[m])
            e0[m, b * step : (b + 1) * step, :] = x
            pk0[b, pl.ds(row, 1), :] = peak
            tt0[b, pl.ds(row, 1), :] = total

    def take_q(s):
        q_copy(s).wait_recv()
        q1[s] = upright(q1t[s].astype(jnp.float32), lanes)

    stats_one(0)
    loads[4].wait()
    q0a[...] = upright(queries_of(nz_ref[...], precision, drift, height), lanes)
    for s in range(0, cols, 2):
        at = pl.multiple_of(flip(c, s, cols) * own, own)
        q0[s // 2 * own : (s // 2 + 1) * own, :] = q0a[pl.ds(at, own), :]
    y_copy = remote(q0.at[pl.ds(0, near)], q0.at[pl.ds(near, near)], y_send.at[0], y_recv.at[0], row_peer(1))
    y_copy.start()
    take_q(1)
    stats_one(1)
    rounds = ready.shape[0]

    def hear(i):
        pl.semaphore_wait(ready.at[i], len(beside))
        if i + 1 < rounds:
            call(ready.at[i + 1])

    hear(0)
    for m in late:
        t_copy(m).start()
    stats_zero(0, 0, blocks // 2)
    for s in far:
        take_q(s)
        stats_one(s)

    def l1_copy(m):
        return remote(l1.at[0], l1.at[m], l1_send.at[0], l1_recv.at[0], row_peer(m))

    for i in range(1, rounds):
        hear(i)
    l1[0] = merged([pk1[s] for s in range(cols)], [tt1[s] for s in range(cols)])
    for m in reversed(range(1, rows)):
        l1_copy(m).start()

    def t_all(first, count):
        view = t1.at[pl.ds(first, count), pl.ds(0, depth)]
        return remote(view, view, t_send.at[0], t_recv.at[first % 2], col_peer(1))

    if rows > 2:
        t_all(2, rows // 2 - 1).wait_recv()
    for m in range(2, rows, 2):
        t_copy(m + 1).start()
    y_copy.wait_recv()
    stats_zero(0, blocks // 2, blocks)
    for m in range(2, rows, 2):
        stats_zero(m, 0, blocks)
    t_all(1, rows // 2).wait_recv()
    for m in range(1, rows, 2):
        stats_zero(m, 0, blocks)
    l0[0] = merged([pk0[b] for b in range(blocks)], [tt0[b] for b in range(blocks)])

    def l0_copy(m):
        return remote(l0.at[0], l0.at[m], l0_send.at[0], l0_recv.at[0], line_peer(m))

    for m in reversed(range(1, rows)):
        l0_copy(m).start()

    def weights_one(s, k):
        return (e1[s, k] * f1[s, k : k + 1, :]).astype(jnp.bfloat16)

    def partial_one(s):
        total = None
        for k in range(chunks):
            part = jnp.dot(
                weights_one(s, k), terminal_ref[k * width : (k + 1) * width, :], preferred_element_type=jnp.float32
            )
            total = part if total is None else total + part
        return total

    def pair_copy(out, into, send, recv, s):
        return remote(out.at[s // 2], into.at[s // 2], send.at[0], recv.at[s // 2], col_peer(1))

    def far_copy(s, h):
        at = h * (cols // 2 - 1) + s // 2 - 1
        piece = pl.ds(h * size, size)
        return remote(
            far_out1.at[s // 2, piece], far_in1.at[s // 2, piece], far1_send.at[0], far1_recv.at[at], col_peer(s)
        )

    def last_copy(s, h):
        piece = pl.ds(h * count, count)
        return remote(far_out0.at[s, piece], far_in0.at[s, piece], far0_send.at[0], far0_recv.at[h], plane_peer(s))

    pair1 = (pair_out1, pair_in1, pair1_send, pair1_recv)
    size = own // PARTS
    count = own // LAST
    away = list(range(2, cols, 2))

    l1_all = remote(l1.at[pl.ds(1, rows - 1)], l1.at[pl.ds(1, rows - 1)], l1_send.at[0], l1_recv.at[0], row_peer(1))
    l1_all.wait_recv()
    loads[5].wait()
    level = merged([l1[m] for m in range(rows)], None)
    for s in range(cols):
        f1[s] = jnp.exp(pk1[s] - level)
    for s in [s + 1 for s in away] + [1] + away + [0]:
        total = partial_one(s)
        if s % 2:
            pair_out1[s // 2] = total
            pair_copy(*pair1, s - 1).start()
        else:
            acc1[s // 2] = total
    for s in away:
        pair_copy(*pair1, s).wait_recv()
        for h in range(PARTS):
            piece = slice(h * size, (h + 1) * size)
            far_out1[s // 2, piece, :] = acc1[s // 2, piece, :] + pair_in1[s // 2, piece, :]
            far_copy(s, h).start()
    pair_copy(*pair1, 0).wait_recv()
    held = acc1[0] + pair_in1[0]
    loads[6].wait()
    loads[7].wait()
    l0_all = remote(l0.at[pl.ds(1, rows - 1)], l0.at[pl.ds(1, rows - 1)], l0_send.at[0], l0_recv.at[0], col_peer(1))
    l0_all.wait_recv()
    level = merged([l0[m] for m in range(rows)], None)
    for b in range(blocks):
        f0[b] = jnp.exp(pk0[b] - level)

    def p_copy(m, h):
        piece = pl.ds(h * size, size)
        if m % 2:
            src, peer, recv = price.at[m - 1, piece], col_peer(1), pc_recv.at[m // 2]
        else:
            recv = p_recv.at[h * (rows // 2 - 1) + m // 2 - 1]
            src, peer = (price.at[m - 2, piece], row_peer(2)) if relayed(m, h) else (price.at[0, piece], row_peer(m))
        return remote(src, price.at[m, piece], p_send.at[0], recv, peer)

    def relayed(m, h):
        return h < RELAY and m % 4 == 2 and m > 2

    def p_core(m):
        return remote(price.at[m], price.at[m], p_send.at[0], pc_recv.at[m // 2], col_peer(1))

    for h in range(PARTS):
        piece = slice(h * size, (h + 1) * size)
        carried = held[piece]
        for s in away:
            far_copy(s, h).wait_recv()
            carried = carried + far_in1[s // 2, piece, :]
        value = settled(flags_ref[1:2, :], ex1_ref[piece, :], carried)
        price[0, piece, :] = value.astype(jnp.bfloat16)
        for m in range(rows - 2, 0, -2):
            if not relayed(m, h):
                p_copy(m, h).start()
        p_copy(1, h).start()
        v1_ref[piece, :] = value
    keep_one = pltpu.make_async_copy(v1_ref, v1_out, local.at[9])
    keep_one.start()

    def add_zero(m, first, count):
        row = flip(group, m, rows)
        parts = []
        each = min(step, count)
        for at in range(first, first + count, each):
            w = (e0[m, at : at + each, :] * f0[at // step, pl.ds(row, 1), :]).astype(jnp.bfloat16)
            parts.append(jnp.dot(w, price[m], preferred_element_type=jnp.float32))
        return parts[0] if len(parts) == 1 else jnp.concatenate(parts, axis=0)

    def gain(m):
        for at in range(0, sources, step):
            part = add_zero(m, at, step)
            acc0[at : at + step, :] = part if m == 0 else acc0[at : at + step, :] + part

    gain(0)
    def pass_on(m, h):
        p_copy(m, h).wait_recv()
        if m + 2 < rows and relayed(m + 2, h) and m % 4 == 0:
            p_copy(m + 2, h).start()
        p_copy(m + 1, h).start()

    direct = [m for m in range(2, rows, 2) if m % 4 == 0 or m == 2]
    other = [m for m in range(2, rows, 2) if m not in direct]
    for h in range(PARTS):
        for m in reversed(direct):
            pass_on(m, h)
        for m in other:
            if not relayed(m, h):
                pass_on(m, h)
    p_core(1).wait_recv()
    for m in [1] + direct:
        gain(m)
    for h in range(min(RELAY, PARTS)):
        for m in other:
            pass_on(m, h)
    for m in other:
        gain(m)
    for m in range(3, rows - 2, 2):
        p_core(m).wait_recv()
        gain(m)
    if rows > 2:
        p_core(rows - 1).wait_recv()
    held = None
    for s in [s + 1 for s in away] + away + [1, 0]:
        at = (s % 2) * near + s // 2 * own
        total = acc0[at : at + own, :] + add_zero(rows - 1, at, own)
        if s:
            far_out0[s] = total.astype(far_out0.dtype)
            for h in range(LAST):
                last_copy(s, h).start()
        else:
            held = total
    loads[8].wait()
    for h in range(LAST):
        piece = slice(h * count, (h + 1) * count)
        carried = held[piece]
        view = far_in0.at[pl.ds(1, cols - 1), pl.ds(h * count, count)]
        remote(view, view, far0_send.at[0], far0_recv.at[h], col_peer(1)).wait_recv()
        for s in range(1, cols):
            carried = carried + far_in0[s, piece, :].astype(jnp.float32)
        v0_ref[piece, :] = settled(flags_ref[0:1, :], ex0_ref[piece, :], carried)
    keep_zero = pltpu.make_async_copy(v0_ref, v0_out, local.at[10])
    keep_zero.start()

    y_copy.wait_send()

    def sent(ref, first, count, sem):
        view = ref.at[pl.ds(first, count)]
        remote(view, view, sem.at[0], y_recv.at[0], col_peer(1)).wait_send()

    sent(q1t, 0, cols - 1, q_send)
    t_all(1, rows - 1).wait_send()
    l1_all.wait_send()
    l0_all.wait_send()
    sent(price, 0, rows - 1, p_send)
    sent(pair_out1, 0, cols // 2, pair1_send)
    if away:
        sent(far_out1, 1, cols // 2 - 1, far1_send)
    sent(far_out0, 1, cols - 1, far0_send)
    keep_one.wait()
    keep_zero.wait()


def shards(rows, cols, nodes_zero, nodes_one, nodes_two, precision, drift, terminal, ex1, ex0, flags):
    own, depth = nodes_one.shape
    height = depth + 16
    sources = nodes_zero.shape[0]
    targets = nodes_two.shape[0]
    trades = terminal.shape[1]
    width = min(TILE, targets)
    chunks = targets // width
    step = max(own, min(TILE, sources))
    blocks = sources // step
    lanes = 128 * (-(-(depth + 3) // 128))
    dma = pltpu.SemaphoreType.DMA
    f32, bf16 = jnp.float32, jnp.bfloat16
    row_stat = pltpu.VMEM((cols, chunks, width), f32)
    col_stat = pltpu.VMEM((blocks, rows, own), f32)
    piece = pltpu.VMEM((cols // 2, own, trades), f32)
    slim = pltpu.VMEM((cols, own, trades), bf16)
    mine = pltpu.VMEM((own, trades), f32)
    one, zero = pl.pallas_call(
        functools.partial(body, rows, cols),
        out_shape=(pltpu.VMEM((own, trades), f32),) * 2,
        in_specs=[pl.BlockSpec(memory_space=pltpu.HBM)] * 9,
        out_specs=(pl.BlockSpec(memory_space=pl.ANY),) * 2,
        scratch_shapes=[
            pltpu.VMEM((1, depth), f32),
            pltpu.VMEM((1, depth), f32),
            pltpu.VMEM((2, trades), jnp.int32),
            pltpu.VMEM((depth, sources), f32),
            pltpu.VMEM((depth, own), f32),
            pltpu.VMEM((depth, targets), f32),
            pltpu.VMEM((targets, trades), bf16),
            *[mine] * 4,
            pltpu.VMEM((cols, height, own), bf16),
            pltpu.VMEM((cols, own, lanes), bf16),
            pltpu.VMEM((rows, lanes, own), bf16),
            pltpu.VMEM((sources, lanes), bf16),
            pltpu.VMEM((sources, lanes), bf16),
            pltpu.VMEM((chunks, lanes, width), bf16),
            pltpu.VMEM((cols, chunks, own, width), f32),
            pltpu.VMEM((rows, sources, own), f32),
            row_stat,
            row_stat,
            row_stat,
            col_stat,
            col_stat,
            col_stat,
            pltpu.VMEM((rows, chunks, width), f32),
            pltpu.VMEM((rows, rows, own), f32),
            pltpu.VMEM((rows, own, trades), bf16),
            piece,
            pltpu.VMEM((sources, trades), f32),
            *[piece] * 4,
            *[slim] * 2,
            dma((1,)),
            dma((cols - 1,)),
            dma((1,)),
            dma((2,)),
            *[dma((1,))] * 5,
            dma((PARTS * max(1, rows // 2 - 1),)),
            dma((rows // 2,)),
            dma((1,)),
            dma((cols // 2,)),
            dma((1,)),
            dma((PARTS * max(1, cols // 2 - 1),)),
            *[dma((1,))] * 3,
            dma((LAST,)),
            dma((11,)),
            pltpu.SemaphoreType.REGULAR((max(1, rows.bit_length() - 2),)),
        ],
        compiler_params=pltpu.CompilerParams(
            collective_id=0, has_side_effects=True, vmem_limit_bytes=LIMIT
        ),
    )(nodes_zero.T, nodes_one.T, nodes_two.T, precision[None, :], drift[None, :], terminal, ex1, ex0, flags)
    return handed(one, zero)


def hand(a, b, c, d, sems):
    copies = [pltpu.make_async_copy(a, c, sems.at[0]), pltpu.make_async_copy(b, d, sems.at[1])]
    for copy in copies:
        copy.start()
    for copy in copies:
        copy.wait()


def handed(one, zero):
    here = pl.BlockSpec(memory_space=pltpu.VMEM)
    out = jax.ShapeDtypeStruct(one.shape, one.dtype)
    return pl.pallas_call(
        hand,
        out_shape=(out, out),
        in_specs=[here, here],
        out_specs=(pl.BlockSpec(memory_space=pltpu.HBM),) * 2,
        scratch_shapes=[pltpu.SemaphoreType.DMA((2,))],
        compiler_params=pltpu.CompilerParams(vmem_limit_bytes=2 * 1024 * 1024),
    )(one, zero)


def solution(mesh):
    both = P(("row", "col"), None)
    return jax.shard_map(
        functools.partial(shards, mesh.shape["row"], mesh.shape["col"]),
        mesh=mesh,
        in_specs=(P("row", None), both, P("col", None), P(), P(), P("col", None), both, both, P()),
        out_specs=(both, both),
        check_vma=False,
    )
```

time: 37.8 us -> 34.6 us (0.915)
  Pallas kernels: 37 us -> 33.8 us
    pallas_call x1, Pallas kernels: 36.3 us -> 33.1 us  [shards(): pl.pallas_call(functools.partial(body, rows, cols), out_shape=(pltpu.VMEM...]
where the time goes in v3:
time: 34.6 us; the launch traced here: 34.5 us
  Pallas kernels  33.8 us (98%)
  between operations  0.64 us (2%)
    pallas_call x1, Pallas kernels, shards(): pl.pallas_call(functools.partial(body, rows, cols), out_shape=(pltpu.VMEM...  33.1 us
    pallas_call x1, Pallas kernels, handed(): pl.pallas_call(hand, out_shape=(out, out), in_specs=[here, here], out_spe...  0.72 us

profile of v3, /device:TPU:0, one launch (start us, length us, event | category | flops | bytes accessed | tf_op | source)
XLA Modules:
  0.0 34.5 jit_solution(15212758846544751777)
XLA Ops:
  0.6 33.1 %shard_map.104 = (f32[256,128]{1,0:T(8,128)S(1)}, f32[256,128]{1,0:T(8,128)S(1)}) custom-call(f32[64,1024]{1,0:T(8,128)} %bitcast.6, f32[64,256]{1,0:T(8,128)} %bitcast.7, f32[64,2048]{1,0:T(8,128)} %bitcast.5, f32[1,64]{1,0:T(1,128)} %bitcast.8, f32[1,64]{1,0:T(1,128)} %bitcast.9, bf16[2048,128]{1,0:T(8,128)(2,1)} %terminal_hbm.1, f32[256,128]{1,0:T(8,128)} %ex1_hbm.1, ...), custom_call_target="tpu_custom_call" | custom-call | tf_op jit(solution)/shard_map/pallas_call | solution.py:517
  33.8 0.7 %shard_map.105 = (f32[256,128]{1,0:T(8,128)}, f32[256,128]{1,0:T(8,128)}) custom-call(f32[256,128]{1,0:T(8,128)S(1)} %get-tuple-element.4.a, f32[256,128]{1,0:T(8,128)S(1)} %get-tuple-element.5.b), custom_call_target="tpu_custom_call" | custom-call | tf_op jit(solution)/shard_map/pallas_call | solution.py:586

commit v4 on v3

--- a/solution.py
+++ b/solution.py
@@ -9,8 +9,9 @@
 
 MESH = pl.DeviceIdType.MESH
 TILE = 256
-PARTS = 2
-RELAY = 1
+PARTS = 4
+RELAY = 2
+CUTS = 2
 LAST = 2
 LIMIT = 60 * 1024 * 1024
 
@@ -178,16 +179,24 @@
             src_ref=src, dst_ref=dst, send_sem=send, recv_sem=recv, device_id=peer, device_id_type=MESH
         )
 
-    beside = [col_peer(s) for s in range(1, cols)]
-    m = 1
-    while m < rows:
-        beside.append(row_peer(m))
-        m *= 2
+    line = rows // 2
+    deep = lax.div(r, 2)
+    core = lax.rem(c, 2)
+    beside = cols + jnp.where(deep > 0, 1, 0) + jnp.where(deep < line - 1, 1, 0)
     barrier = pltpu.get_barrier_semaphore()
 
     def call(sem):
-        for peer in beside:
-            pl.semaphore_signal(sem, inc=1, device_id=peer, device_id_type=MESH)
+        for s in range(1, cols):
+            pl.semaphore_signal(sem, inc=1, device_id=col_peer(s), device_id_type=MESH)
+        pl.semaphore_signal(sem, inc=1, device_id=row_peer(1), device_id_type=MESH)
+
+        @pl.when(deep > 0)
+        def _():
+            pl.semaphore_signal(sem, inc=1, device_id=(r - 2, c), device_id_type=MESH)
+
+        @pl.when(deep < line - 1)
+        def _():
+            pl.semaphore_signal(sem, inc=1, device_id=(r + 2, c), device_id_type=MESH)
 
     call(barrier)
     loads = [
@@ -215,28 +224,28 @@
     mine = queries_of(n1_ref[...], precision, drift, height)
     q1t[0] = mine.astype(jnp.bfloat16)
     t1[0, :depth, :] = n1_ref[...].astype(jnp.bfloat16)
-    pl.semaphore_wait(barrier, len(beside))
+    pl.semaphore_wait(barrier, beside)
     call(ready.at[0])
 
-    def q_copy(s):
-        return remote(q1t.at[0], q1t.at[s], q_send.at[0], q_recv.at[s - 1], col_peer(s))
-
-    far = list(range(2, cols, 2)) + list(range(3, cols, 2))
-    for s in [1] + far:
-        q_copy(s).start()
+    def q_copy(s, peer):
+        return remote(q1t.at[0], q1t.at[s], q_send.at[0], q_recv.at[s - 1], peer)
+
+    q_copy(1, col_peer(1)).start()
+    for other in range(2):
+        for s in range(2, cols, 2):
+            slot = s + (1 - core if other else core)
+            q_copy(slot, (r, flip(c, s, cols) - core + other)).start()
 
     def t_copy(m):
         if m % 2:
             src, peer = t1.at[m - 1, pl.ds(0, depth)], col_peer(1)
         else:
             src, peer = t1.at[0, pl.ds(0, depth)], row_peer(m)
-        return remote(src, t1.at[m, pl.ds(0, depth)], t_send.at[0], t_recv.at[m % 2], peer)
+        return remote(src, t1.at[m, pl.ds(0, depth)], t_send.at[0], t_recv.at[m % 2 + (2 if m >= 6 else 0)], peer)
 
     t_copy(1).start()
-    soon = [m for m in range(2, rows, 2) if m & (m - 1) == 0]
-    late = [m for m in range(2, rows, 2) if m & (m - 1)]
-    for m in soon:
-        t_copy(m).start()
+    if rows > 2:
+        t_copy(2).start()
 
     q1[0] = upright(mine, lanes)
     for m in range(rows):
@@ -250,8 +259,8 @@
         for k in range(chunks):
             x, peak, total = scored(q1[s], t2[k])
             e1[s, k] = x
-            pk1[s, k : k + 1, :] = peak
-            tt1[s, k : k + 1, :] = total
+            pk1[s, pl.ds(k, 1), :] = peak
+            tt1[s, pl.ds(k, 1), :] = total
 
     def stats_zero(m, first, last):
         row = flip(group, m, rows)
@@ -262,7 +271,7 @@
             tt0[b, pl.ds(row, 1), :] = total
 
     def take_q(s):
-        q_copy(s).wait_recv()
+        q_copy(s, col_peer(1)).wait_recv()
         q1[s] = upright(q1t[s].astype(jnp.float32), lanes)
 
     stats_one(0)
@@ -273,69 +282,80 @@
         q0[s // 2 * own : (s // 2 + 1) * own, :] = q0a[pl.ds(at, own), :]
     y_copy = remote(q0.at[pl.ds(0, near)], q0.at[pl.ds(near, near)], y_send.at[0], y_recv.at[0], row_peer(1))
     y_copy.start()
+    rounds = ready.shape[0]
+
+    def hear(i):
+        pl.semaphore_wait(ready.at[i], beside)
+        if i + 1 < rounds:
+            call(ready.at[i + 1])
+
     take_q(1)
     stats_one(1)
-    rounds = ready.shape[0]
-
-    def hear(i):
-        pl.semaphore_wait(ready.at[i], len(beside))
-        if i + 1 < rounds:
-            call(ready.at[i + 1])
-
+    stats_zero(0, 0, blocks // 2)
     hear(0)
-    for m in late:
-        t_copy(m).start()
-    stats_zero(0, 0, blocks // 2)
-    for s in far:
-        take_q(s)
-        stats_one(s)
+    if rows > 4:
+        t_copy(4).start()
+    for other in range(2):
+        for s in range(2, cols, 2):
+            slot = s + (core if other else 1 - core)
+            take_q(slot)
+            stats_one(slot)
+        if other == 0:
+            for i in range(1, rounds - 1):
+                hear(i)
+            for m in range(6, rows, 2):
+                t_copy(m).start()
 
     def l1_copy(m):
         return remote(l1.at[0], l1.at[m], l1_send.at[0], l1_recv.at[0], row_peer(m))
 
-    for i in range(1, rounds):
-        hear(i)
+    if rounds > 1:
+        hear(rounds - 1)
     l1[0] = merged([pk1[s] for s in range(cols)], [tt1[s] for s in range(cols)])
     for m in reversed(range(1, rows)):
         l1_copy(m).start()
 
-    def t_all(first, count):
-        view = t1.at[pl.ds(first, count), pl.ds(0, depth)]
-        return remote(view, view, t_send.at[0], t_recv.at[first % 2], col_peer(1))
-
-    if rows > 2:
-        t_all(2, rows // 2 - 1).wait_recv()
-    for m in range(2, rows, 2):
-        t_copy(m + 1).start()
+    def t_all(count, at):
+        view = t1.at[pl.ds(0, count), pl.ds(0, depth)]
+        return remote(view, view, t_send.at[0], t_recv.at[at], col_peer(1))
+
+    first_ones, late_ones = range(2, min(6, rows), 2), range(6, rows, 2)
+    if first_ones:
+        t_all(len(first_ones), 0).wait_recv()
+        for m in first_ones:
+            t_copy(m + 1).start()
     y_copy.wait_recv()
     stats_zero(0, blocks // 2, blocks)
-    for m in range(2, rows, 2):
+    for m in first_ones:
         stats_zero(m, 0, blocks)
-    t_all(1, rows // 2).wait_recv()
-    for m in range(1, rows, 2):
+    t_all(1 + len(first_ones), 1).wait_recv()
+    if late_ones:
+        t_all(len(late_ones), 2).wait_recv()
+        for m in late_ones:
+            t_copy(m + 1).start()
+    for m in [1] + [m + 1 for m in first_ones]:
         stats_zero(m, 0, blocks)
-    l0[0] = merged([pk0[b] for b in range(blocks)], [tt0[b] for b in range(blocks)])
-
-    def l0_copy(m):
-        return remote(l0.at[0], l0.at[m], l0_send.at[0], l0_recv.at[0], line_peer(m))
-
-    for m in reversed(range(1, rows)):
-        l0_copy(m).start()
-
-    def weights_one(s, k):
-        return (e1[s, k] * f1[s, k : k + 1, :]).astype(jnp.bfloat16)
-
-    def partial_one(s):
+
+    def weights_one(s, k, first, many):
+        return (e1[s, k, first : first + many, :] * f1[s, k : k + 1, :]).astype(jnp.bfloat16)
+
+    def partial_one(s, first, many):
         total = None
         for k in range(chunks):
             part = jnp.dot(
-                weights_one(s, k), terminal_ref[k * width : (k + 1) * width, :], preferred_element_type=jnp.float32
+                weights_one(s, k, first, many), terminal_ref[k * width : (k + 1) * width, :], preferred_element_type=jnp.float32
             )
             total = part if total is None else total + part
         return total
 
-    def pair_copy(out, into, send, recv, s):
-        return remote(out.at[s // 2], into.at[s // 2], send.at[0], recv.at[s // 2], col_peer(1))
+    cut = own // CUTS
+
+    def pair_copy(s, h):
+        piece = pl.ds(h * cut, cut)
+        at = h * (cols // 2) + s // 2
+        return remote(
+            pair_out1.at[s // 2, piece], pair_in1.at[s // 2, piece], pair1_send.at[0], pair1_recv.at[at], col_peer(1)
+        )
 
     def far_copy(s, h):
         at = h * (cols // 2 - 1) + s // 2 - 1
@@ -348,7 +368,6 @@
         piece = pl.ds(h * count, count)
         return remote(far_out0.at[s, piece], far_in0.at[s, piece], far0_send.at[0], far0_recv.at[h], plane_peer(s))
 
-    pair1 = (pair_out1, pair_in1, pair1_send, pair1_recv)
     size = own // PARTS
     count = own // LAST
     away = list(range(2, cols, 2))
@@ -359,28 +378,43 @@
     level = merged([l1[m] for m in range(rows)], None)
     for s in range(cols):
         f1[s] = jnp.exp(pk1[s] - level)
-    for s in [s + 1 for s in away] + [1] + away + [0]:
-        total = partial_one(s)
-        if s % 2:
-            pair_out1[s // 2] = total
-            pair_copy(*pair1, s - 1).start()
-        else:
-            acc1[s // 2] = total
+    def give(s):
+        for h in range(CUTS):
+            pair_out1[s // 2, h * cut : (h + 1) * cut, :] = partial_one(s + 1, h * cut, cut)
+            pair_copy(s, h).start()
+
     for s in away:
-        pair_copy(*pair1, s).wait_recv()
-        for h in range(PARTS):
-            piece = slice(h * size, (h + 1) * size)
-            far_out1[s // 2, piece, :] = acc1[s // 2, piece, :] + pair_in1[s // 2, piece, :]
-            far_copy(s, h).start()
-    pair_copy(*pair1, 0).wait_recv()
+        give(s)
+    for s in away:
+        acc1[s // 2] = partial_one(s, 0, own)
+    give(0)
+    for h in range(CUTS):
+        for s in away:
+            pair_copy(s, h).wait_recv()
+            for i in range(h * PARTS // CUTS, (h + 1) * PARTS // CUTS):
+                piece = slice(i * size, (i + 1) * size)
+                far_out1[s // 2, piece, :] = acc1[s // 2, piece, :] + pair_in1[s // 2, piece, :]
+                far_copy(s, i).start()
+    acc1[0] = partial_one(0, 0, own)
+    for h in range(CUTS):
+        pair_copy(0, h).wait_recv()
     held = acc1[0] + pair_in1[0]
+    for m in late_ones:
+        stats_zero(m, 0, blocks)
+    if late_ones:
+        t_all(len(late_ones), 3).wait_recv()
+    for m in late_ones:
+        stats_zero(m + 1, 0, blocks)
+    l0[0] = merged([pk0[b] for b in range(blocks)], [tt0[b] for b in range(blocks)])
+
+    def l0_copy(m):
+        return remote(l0.at[0], l0.at[m], l0_send.at[0], l0_recv.at[0], line_peer(m))
+
+    for m in reversed(range(1, rows)):
+        l0_copy(m).start()
+
     loads[6].wait()
     loads[7].wait()
-    l0_all = remote(l0.at[pl.ds(1, rows - 1)], l0.at[pl.ds(1, rows - 1)], l0_send.at[0], l0_recv.at[0], col_peer(1))
-    l0_all.wait_recv()
-    level = merged([l0[m] for m in range(rows)], None)
-    for b in range(blocks):
-        f0[b] = jnp.exp(pk0[b] - level)
 
     def p_copy(m, h):
         piece = pl.ds(h * size, size)
@@ -412,9 +446,7 @@
         v1_ref[piece, :] = value
     keep_one = pltpu.make_async_copy(v1_ref, v1_out, local.at[9])
     keep_one.start()
-
-    def add_zero(m, first, count):
-        row = flip(group, m, rows)
+    def add_zero(m, row, first, count):
         parts = []
         each = min(step, count)
         for at in range(first, first + count, each):
@@ -422,17 +454,26 @@
             parts.append(jnp.dot(w, price[m], preferred_element_type=jnp.float32))
         return parts[0] if len(parts) == 1 else jnp.concatenate(parts, axis=0)
 
-    def gain(m):
+    def gain(slots):
         for at in range(0, sources, step):
-            part = add_zero(m, at, step)
-            acc0[at : at + step, :] = part if m == 0 else acc0[at : at + step, :] + part
-
-    gain(0)
+            total = acc0[at : at + step, :] if 0 not in slots else None
+            for m in slots:
+                part = add_zero(m, flip(group, m, rows), at, step)
+                total = part if total is None else total + part
+            acc0[at : at + step, :] = total
+
     def pass_on(m, h):
         p_copy(m, h).wait_recv()
         if m + 2 < rows and relayed(m + 2, h) and m % 4 == 0:
             p_copy(m + 2, h).start()
         p_copy(m + 1, h).start()
+
+    def ready_zero():
+        l0_all = remote(l0.at[pl.ds(1, rows - 1)], l0.at[pl.ds(1, rows - 1)], l0_send.at[0], l0_recv.at[0], col_peer(1))
+        l0_all.wait_recv()
+        level = merged([l0[m] for m in range(rows)], None)
+        for b in range(blocks):
+            f0[b] = jnp.exp(pk0[b] - level)
 
     direct = [m for m in range(2, rows, 2) if m % 4 == 0 or m == 2]
     other = [m for m in range(2, rows, 2) if m not in direct]
@@ -442,23 +483,42 @@
         for m in other:
             if not relayed(m, h):
                 pass_on(m, h)
-    p_core(1).wait_recv()
-    for m in [1] + direct:
-        gain(m)
+        if h == PARTS // 2 - 1:
+            ready_zero()
+            p_core(1).wait_recv()
+            gain([0, 1])
+    gain(direct)
     for h in range(min(RELAY, PARTS)):
         for m in other:
             pass_on(m, h)
-    for m in other:
-        gain(m)
-    for m in range(3, rows - 2, 2):
+    ahead = [m for m in range(3, rows - 2, 2)]
+    for m in ahead:
         p_core(m).wait_recv()
-        gain(m)
-    if rows > 2:
-        p_core(rows - 1).wait_recv()
+    if ahead:
+        gain(ahead)
+
+    @pl.when(core == 0)
+    def _():
+        if rows > 2:
+            p_core(rows - 1).wait_recv()
+        if other:
+            gain(other[:-1] + [rows - 1])
+
+    @pl.when(core == 1)
+    def _():
+        if other:
+            gain(other)
+        if rows > 2:
+            p_core(rows - 1).wait_recv()
+
+    if other:
+        final, final_row = rows - 2 + core, flip(group, rows - 2, rows) - core
+    else:
+        final, final_row = rows - 1, flip(group, rows - 1, rows)
     held = None
     for s in [s + 1 for s in away] + away + [1, 0]:
         at = (s % 2) * near + s // 2 * own
-        total = acc0[at : at + own, :] + add_zero(rows - 1, at, own)
+        total = acc0[at : at + own, :] + add_zero(final, final_row, at, own)
         if s:
             far_out0[s] = total.astype(far_out0.dtype)
             for h in range(LAST):
@@ -484,9 +544,9 @@
         remote(view, view, sem.at[0], y_recv.at[0], col_peer(1)).wait_send()
 
     sent(q1t, 0, cols - 1, q_send)
-    t_all(1, rows - 1).wait_send()
+    t_all(rows - 1, 0).wait_send()
     l1_all.wait_send()
-    l0_all.wait_send()
+    remote(l0.at[pl.ds(1, rows - 1)], l0.at[pl.ds(1, rows - 1)], l0_send.at[0], l0_recv.at[0], col_peer(1)).wait_send()
     sent(price, 0, rows - 1, p_send)
     sent(pair_out1, 0, cols // 2, pair1_send)
     if away:
@@ -552,18 +612,18 @@
             dma((1,)),
             dma((cols - 1,)),
             dma((1,)),
-            dma((2,)),
+            dma((4,)),
             *[dma((1,))] * 5,
             dma((PARTS * max(1, rows // 2 - 1),)),
             dma((rows // 2,)),
             dma((1,)),
-            dma((cols // 2,)),
+            dma((CUTS * (cols // 2),)),
             dma((1,)),
             dma((PARTS * max(1, cols // 2 - 1),)),
             *[dma((1,))] * 3,
             dma((LAST,)),
             dma((11,)),
-            pltpu.SemaphoreType.REGULAR((max(1, rows.bit_length() - 2),)),
+            pltpu.SemaphoreType.REGULAR((max(1, rows // 2 - 1),)),
         ],
         compiler_params=pltpu.CompilerParams(
             collective_id=0, has_side_effects=True, vmem_limit_bytes=LIMIT

time: 34.6 us -> 33.7 us (0.974)
  Pallas kernels: 33.8 us -> 33 us
    pallas_call x1, Pallas kernels: 33.1 us -> 32.2 us  [shards(): pl.pallas_call(functools.partial(body, rows, cols), out_shape=(pltpu.VMEM...]
where the time goes in v4:
time: 33.7 us; the launch traced here: 33.6 us
  Pallas kernels  33 us (98%)
  between operations  0.64 us (2%)
    pallas_call x1, Pallas kernels, shards(): pl.pallas_call(functools.partial(body, rows, cols), out_shape=(pltpu.VMEM...  32.2 us
    pallas_call x1, Pallas kernels, handed(): pl.pallas_call(hand, out_shape=(out, out), in_specs=[here, here], out_spe...  0.72 us

profile of v4, /device:TPU:0, one launch (start us, length us, event | category | flops | bytes accessed | tf_op | source)
XLA Modules:
  0.0 33.6 jit_solution(9964626634758495740)
XLA Ops:
  0.6 32.2 %shard_map.104 = (f32[256,128]{1,0:T(8,128)S(1)}, f32[256,128]{1,0:T(8,128)S(1)}) custom-call(f32[64,1024]{1,0:T(8,128)} %bitcast.6, f32[64,256]{1,0:T(8,128)} %bitcast.7, f32[64,2048]{1,0:T(8,128)} %bitcast.5, f32[1,64]{1,0:T(1,128)} %bitcast.8, f32[1,64]{1,0:T(1,128)} %bitcast.9, bf16[2048,128]{1,0:T(8,128)(2,1)} %terminal_hbm.1, f32[256,128]{1,0:T(8,128)} %ex1_hbm.1, ...), custom_call_target="tpu_custom_call" | custom-call | tf_op jit(solution)/shard_map/pallas_call | solution.py:577
  32.9 0.7 %shard_map.105 = (f32[256,128]{1,0:T(8,128)}, f32[256,128]{1,0:T(8,128)}) custom-call(f32[256,128]{1,0:T(8,128)S(1)} %get-tuple-element.4.a, f32[256,128]{1,0:T(8,128)S(1)} %get-tuple-element.5.b), custom_call_target="tpu_custom_call" | custom-call | tf_op jit(solution)/shard_map/pallas_call | solution.py:646

commit v5 on v4

--- a/solution.py
+++ b/solution.py
@@ -117,6 +117,7 @@
     tt0,
     f0,
     l1,
+    l0p,
     l0,
     price,
     acc1,
@@ -133,6 +134,8 @@
     t_recv,
     l1_send,
     l1_recv,
+    l0p_send,
+    l0p_recv,
     l0_send,
     l0_recv,
     p_send,
@@ -168,9 +171,6 @@
     def col_peer(s):
         return (r, flip(c, s, cols))
 
-    def line_peer(m):
-        return (flip(r, m - m % 2, rows), flip(c, m % 2, cols))
-
     def plane_peer(s):
         return (flip(r, s % 2, rows), flip(c, s - s % 2, cols))
 
@@ -290,21 +290,21 @@
             call(ready.at[i + 1])
 
     take_q(1)
-    stats_one(1)
-    stats_zero(0, 0, blocks // 2)
     hear(0)
     if rows > 4:
         t_copy(4).start()
+    stats_one(1)
+    stats_zero(0, 0, blocks // 2)
     for other in range(2):
         for s in range(2, cols, 2):
             slot = s + (core if other else 1 - core)
             take_q(slot)
+            if other == 0 and s == 2:
+                for i in range(1, rounds - 1):
+                    hear(i)
+                for m in range(6, rows, 2):
+                    t_copy(m).start()
             stats_one(slot)
-        if other == 0:
-            for i in range(1, rounds - 1):
-                hear(i)
-            for m in range(6, rows, 2):
-                t_copy(m).start()
 
     def l1_copy(m):
         return remote(l1.at[0], l1.at[m], l1_send.at[0], l1_recv.at[0], row_peer(m))
@@ -378,16 +378,19 @@
     level = merged([l1[m] for m in range(rows)], None)
     for s in range(cols):
         f1[s] = jnp.exp(pk1[s] - level)
+    def give_cut(s, h):
+        pair_out1[s // 2, h * cut : (h + 1) * cut, :] = partial_one(s + 1, h * cut, cut)
+        pair_copy(s, h).start()
+
     def give(s):
         for h in range(CUTS):
-            pair_out1[s // 2, h * cut : (h + 1) * cut, :] = partial_one(s + 1, h * cut, cut)
-            pair_copy(s, h).start()
+            give_cut(s, h)
 
     for s in away:
         give(s)
     for s in away:
         acc1[s // 2] = partial_one(s, 0, own)
-    give(0)
+    give_cut(0, 0)
     for h in range(CUTS):
         for s in away:
             pair_copy(s, h).wait_recv()
@@ -395,24 +398,29 @@
                 piece = slice(i * size, (i + 1) * size)
                 far_out1[s // 2, piece, :] = acc1[s // 2, piece, :] + pair_in1[s // 2, piece, :]
                 far_copy(s, i).start()
-    acc1[0] = partial_one(0, 0, own)
-    for h in range(CUTS):
-        pair_copy(0, h).wait_recv()
-    held = acc1[0] + pair_in1[0]
+    for h in range(1, CUTS):
+        give_cut(0, h)
     for m in late_ones:
         stats_zero(m, 0, blocks)
     if late_ones:
         t_all(len(late_ones), 3).wait_recv()
     for m in late_ones:
         stats_zero(m + 1, 0, blocks)
-    l0[0] = merged([pk0[b] for b in range(blocks)], [tt0[b] for b in range(blocks)])
+    l0p[0] = merged([pk0[b] for b in range(blocks)], [tt0[b] for b in range(blocks)])
+    l0_pair = remote(l0p.at[0], l0p.at[1], l0p_send.at[0], l0p_recv.at[0], col_peer(1))
+    l0_pair.start()
+    acc1[0] = partial_one(0, 0, own)
+    for h in range(CUTS):
+        pair_copy(0, h).wait_recv()
+    held = acc1[0] + pair_in1[0]
+    l0_pair.wait_recv()
+    l0[0] = merged([l0p[0], l0p[1]], None)
 
     def l0_copy(m):
-        return remote(l0.at[0], l0.at[m], l0_send.at[0], l0_recv.at[0], line_peer(m))
-
-    for m in reversed(range(1, rows)):
+        return remote(l0.at[0], l0.at[m // 2], l0_send.at[0], l0_recv.at[0], row_peer(m))
+
+    for m in reversed(range(2, rows, 2)):
         l0_copy(m).start()
-
     loads[6].wait()
     loads[7].wait()
 
@@ -468,10 +476,14 @@
             p_copy(m + 2, h).start()
         p_copy(m + 1, h).start()
 
+    def l0_all():
+        view = l0.at[pl.ds(1, rows // 2 - 1)]
+        return remote(view, view, l0_send.at[0], l0_recv.at[0], row_peer(1))
+
     def ready_zero():
-        l0_all = remote(l0.at[pl.ds(1, rows - 1)], l0.at[pl.ds(1, rows - 1)], l0_send.at[0], l0_recv.at[0], col_peer(1))
-        l0_all.wait_recv()
-        level = merged([l0[m] for m in range(rows)], None)
+        if rows > 2:
+            l0_all().wait_recv()
+        level = merged([l0[i] for i in range(rows // 2)], None)
         for b in range(blocks):
             f0[b] = jnp.exp(pk0[b] - level)
 
@@ -546,7 +558,9 @@
     sent(q1t, 0, cols - 1, q_send)
     t_all(rows - 1, 0).wait_send()
     l1_all.wait_send()
-    remote(l0.at[pl.ds(1, rows - 1)], l0.at[pl.ds(1, rows - 1)], l0_send.at[0], l0_recv.at[0], col_peer(1)).wait_send()
+    l0_pair.wait_send()
+    if rows > 2:
+        l0_all().wait_send()
     sent(price, 0, rows - 1, p_send)
     sent(pair_out1, 0, cols // 2, pair1_send)
     if away:
@@ -603,7 +617,8 @@
             col_stat,
             col_stat,
             pltpu.VMEM((rows, chunks, width), f32),
-            pltpu.VMEM((rows, rows, own), f32),
+            pltpu.VMEM((2, rows, own), f32),
+            pltpu.VMEM((rows // 2, rows, own), f32),
             pltpu.VMEM((rows, own, trades), bf16),
             piece,
             pltpu.VMEM((sources, trades), f32),
@@ -613,7 +628,7 @@
             dma((cols - 1,)),
             dma((1,)),
             dma((4,)),
-            *[dma((1,))] * 5,
+            *[dma((1,))] * 7,
             dma((PARTS * max(1, rows // 2 - 1),)),
             dma((rows // 2,)),
             dma((1,)),

time: 33.7 us -> 33.3 us (0.988)
  Pallas kernels: 33 us -> 32.5 us
    pallas_call x1, Pallas kernels: 32.2 us -> 31.8 us  [shards(): pl.pallas_call(functools.partial(body, rows, cols), out_shape=(pltpu.VMEM...]
where the time goes in v5:
time: 33.3 us; the launch traced here: 33.2 us
  Pallas kernels  32.5 us (98%)
  between operations  0.64 us (2%)
    pallas_call x1, Pallas kernels, shards(): pl.pallas_call(functools.partial(body, rows, cols), out_shape=(pltpu.VMEM...  31.8 us
    pallas_call x1, Pallas kernels, handed(): pl.pallas_call(hand, out_shape=(out, out), in_specs=[here, here], out_spe...  0.72 us

profile of v5, /device:TPU:0, one launch (start us, length us, event | category | flops | bytes accessed | tf_op | source)
XLA Modules:
  0.0 33.2 jit_solution(14518193508755644104)
XLA Ops:
  0.6 31.8 %shard_map.104 = (f32[256,128]{1,0:T(8,128)S(1)}, f32[256,128]{1,0:T(8,128)S(1)}) custom-call(f32[64,1024]{1,0:T(8,128)} %bitcast.6, f32[64,256]{1,0:T(8,128)} %bitcast.7, f32[64,2048]{1,0:T(8,128)} %bitcast.5, f32[1,64]{1,0:T(1,128)} %bitcast.8, f32[1,64]{1,0:T(1,128)} %bitcast.9, bf16[2048,128]{1,0:T(8,128)(2,1)} %terminal_hbm.1, f32[256,128]{1,0:T(8,128)} %ex1_hbm.1, ...), custom_call_target="tpu_custom_call" | custom-call | tf_op jit(solution)/shard_map/pallas_call | solution.py:591
  32.4 0.7 %shard_map.105 = (f32[256,128]{1,0:T(8,128)}, f32[256,128]{1,0:T(8,128)}) custom-call(f32[256,128]{1,0:T(8,128)S(1)} %get-tuple-element.4.a, f32[256,128]{1,0:T(8,128)S(1)} %get-tuple-element.5.b), custom_call_target="tpu_custom_call" | custom-call | tf_op jit(solution)/shard_map/pallas_call | solution.py:661

commit v6 on v5

--- a/solution.py
+++ b/solution.py
@@ -10,7 +10,7 @@
 MESH = pl.DeviceIdType.MESH
 TILE = 256
 PARTS = 4
-RELAY = 2
+RELAY = 1
 CUTS = 2
 LAST = 2
 LIMIT = 60 * 1024 * 1024
@@ -54,8 +54,28 @@
     return jnp.where(at < 3, -1.0, 0.0).astype(jnp.bfloat16)
 
 
-def settled(allowed, exercise, carried):
-    return jnp.where(allowed == 1, jnp.maximum(exercise, carried), carried)
+def turned(x):
+    mid = x.shape[1] // 2
+    return jnp.concatenate([x[:, mid:], x[:, :mid]], axis=1)
+
+
+def mixed(a, b):
+    low = lax.broadcasted_iota(jnp.int32, a.shape, 1) < a.shape[1] // 2
+    return jnp.where(low, a, b)
+
+
+def packed(x):
+    top, bottom = x[: x.shape[0] // 2], turned(x[x.shape[0] // 2 :])
+    return jnp.concatenate([mixed(top, bottom), mixed(bottom, top)], axis=0)
+
+
+def unpacked(x):
+    a, b = x[: x.shape[0] // 2], x[x.shape[0] // 2 :]
+    return jnp.concatenate([mixed(a, b), turned(mixed(b, a))], axis=0)
+
+
+def floor_of(allowed, exercise):
+    return packed(jnp.where(allowed == 1, exercise, -jnp.inf))
 
 
 def scored(queries, targets):
@@ -107,6 +127,7 @@
     t1,
     q0a,
     q0,
+    wz,
     t2,
     e1,
     e0,
@@ -155,14 +176,16 @@
     r = lax.axis_index("row")
     c = lax.axis_index("col")
     depth, own = n1_ref.shape
-    lanes = q0.shape[1]
+    lanes = q0a.shape[1]
     height = q1t.shape[1]
     _, chunks, _, width = e1.shape
     trades = price.shape[2]
-    sources = q0.shape[0]
+    sources = q0a.shape[0]
     blocks, _, _ = pk0.shape
     step = sources // blocks
+    half_own = own // 2
     near = sources // 2
+    quarter = sources // 4
     group = 2 * lax.div(r, 2) + lax.rem(c, 2)
 
     def row_peer(m):
@@ -262,10 +285,12 @@
             pk1[s, pl.ds(k, 1), :] = peak
             tt1[s, pl.ds(k, 1), :] = total
 
-    def stats_zero(m, first, last):
+    every = (0, 1, 2, 3)
+
+    def stats_zero(m, which):
         row = flip(group, m, rows)
-        for b in range(first, last):
-            x, peak, total = scored(q0[b * step : (b + 1) * step, :], t1[m])
+        for b in which:
+            x, peak, total = scored(q0[b // 2, b % 2], t1[m])
             e0[m, b * step : (b + 1) * step, :] = x
             pk0[b, pl.ds(row, 1), :] = peak
             tt0[b, pl.ds(row, 1), :] = total
@@ -279,8 +304,9 @@
     q0a[...] = upright(queries_of(nz_ref[...], precision, drift, height), lanes)
     for s in range(0, cols, 2):
         at = pl.multiple_of(flip(c, s, cols) * own, own)
-        q0[s // 2 * own : (s // 2 + 1) * own, :] = q0a[pl.ds(at, own), :]
-    y_copy = remote(q0.at[pl.ds(0, near)], q0.at[pl.ds(near, near)], y_send.at[0], y_recv.at[0], row_peer(1))
+        for side in range(2):
+            q0[side, 0, s // 2 * half_own : (s // 2 + 1) * half_own, :] = q0a[pl.ds(at + side * half_own, half_own), :]
+    y_copy = remote(q0.at[:, 0], q0.at[:, 1], y_send.at[0], y_recv.at[0], row_peer(1))
     y_copy.start()
     rounds = ready.shape[0]
 
@@ -294,7 +320,7 @@
     if rows > 4:
         t_copy(4).start()
     stats_one(1)
-    stats_zero(0, 0, blocks // 2)
+    stats_zero(0, (0, 2))
     for other in range(2):
         for s in range(2, cols, 2):
             slot = s + (core if other else 1 - core)
@@ -325,28 +351,28 @@
         for m in first_ones:
             t_copy(m + 1).start()
     y_copy.wait_recv()
-    stats_zero(0, blocks // 2, blocks)
+    stats_zero(0, (1, 3))
     for m in first_ones:
-        stats_zero(m, 0, blocks)
+        stats_zero(m, every)
     t_all(1 + len(first_ones), 1).wait_recv()
     if late_ones:
         t_all(len(late_ones), 2).wait_recv()
         for m in late_ones:
             t_copy(m + 1).start()
     for m in [1] + [m + 1 for m in first_ones]:
-        stats_zero(m, 0, blocks)
-
-    def weights_one(s, k, first, many):
-        return (e1[s, k, first : first + many, :] * f1[s, k : k + 1, :]).astype(jnp.bfloat16)
-
-    def partial_one(s, first, many):
+        stats_zero(m, every)
+
+    def weights_one(s, k):
+        return (e1[s, k] * f1[s, k : k + 1, :]).astype(jnp.bfloat16)
+
+    def partial_one(s):
         total = None
         for k in range(chunks):
             part = jnp.dot(
-                weights_one(s, k, first, many), terminal_ref[k * width : (k + 1) * width, :], preferred_element_type=jnp.float32
+                weights_one(s, k), terminal_ref[k * width : (k + 1) * width, :], preferred_element_type=jnp.float32
             )
             total = part if total is None else total + part
-        return total
+        return packed(total)
 
     cut = own // CUTS
 
@@ -378,19 +404,18 @@
     level = merged([l1[m] for m in range(rows)], None)
     for s in range(cols):
         f1[s] = jnp.exp(pk1[s] - level)
-    def give_cut(s, h):
-        pair_out1[s // 2, h * cut : (h + 1) * cut, :] = partial_one(s + 1, h * cut, cut)
-        pair_copy(s, h).start()
 
     def give(s):
+        total = partial_one(s + 1)
         for h in range(CUTS):
-            give_cut(s, h)
+            pair_out1[s // 2, h * cut : (h + 1) * cut, :] = total[h * cut : (h + 1) * cut]
+            pair_copy(s, h).start()
 
     for s in away:
         give(s)
     for s in away:
-        acc1[s // 2] = partial_one(s, 0, own)
-    give_cut(0, 0)
+        acc1[s // 2] = partial_one(s)
+    give(0)
     for h in range(CUTS):
         for s in away:
             pair_copy(s, h).wait_recv()
@@ -398,18 +423,20 @@
                 piece = slice(i * size, (i + 1) * size)
                 far_out1[s // 2, piece, :] = acc1[s // 2, piece, :] + pair_in1[s // 2, piece, :]
                 far_copy(s, i).start()
-    for h in range(1, CUTS):
-        give_cut(0, h)
     for m in late_ones:
-        stats_zero(m, 0, blocks)
+        stats_zero(m, every)
     if late_ones:
         t_all(len(late_ones), 3).wait_recv()
     for m in late_ones:
-        stats_zero(m + 1, 0, blocks)
+        stats_zero(m + 1, every)
     l0p[0] = merged([pk0[b] for b in range(blocks)], [tt0[b] for b in range(blocks)])
     l0_pair = remote(l0p.at[0], l0p.at[1], l0p_send.at[0], l0p_recv.at[0], col_peer(1))
     l0_pair.start()
-    acc1[0] = partial_one(0, 0, own)
+    acc1[0] = partial_one(0)
+    for load in loads[6:]:
+        load.wait()
+    ex1_ref[...] = floor_of(flags_ref[1:2, :], ex1_ref[...])
+    ex0_ref[...] = floor_of(flags_ref[0:1, :], ex0_ref[...])
     for h in range(CUTS):
         pair_copy(0, h).wait_recv()
     held = acc1[0] + pair_in1[0]
@@ -421,13 +448,11 @@
 
     for m in reversed(range(2, rows, 2)):
         l0_copy(m).start()
-    loads[6].wait()
-    loads[7].wait()
 
     def p_copy(m, h):
         piece = pl.ds(h * size, size)
         if m % 2:
-            src, peer, recv = price.at[m - 1, piece], col_peer(1), pc_recv.at[m // 2]
+            src, peer, recv = price.at[m - 1, piece], col_peer(1), pc_recv.at[h * 2 // PARTS * line + m // 2]
         else:
             recv = p_recv.at[h * (rows // 2 - 1) + m // 2 - 1]
             src, peer = (price.at[m - 2, piece], row_peer(2)) if relayed(m, h) else (price.at[0, piece], row_peer(m))
@@ -436,8 +461,9 @@
     def relayed(m, h):
         return h < RELAY and m % 4 == 2 and m > 2
 
-    def p_core(m):
-        return remote(price.at[m], price.at[m], p_send.at[0], pc_recv.at[m // 2], col_peer(1))
+    def p_core(m, half):
+        view = price.at[m, pl.ds(half * half_own, half_own)]
+        return remote(view, view, p_send.at[0], pc_recv.at[half * line + m // 2], col_peer(1))
 
     for h in range(PARTS):
         piece = slice(h * size, (h + 1) * size)
@@ -445,30 +471,63 @@
         for s in away:
             far_copy(s, h).wait_recv()
             carried = carried + far_in1[s // 2, piece, :]
-        value = settled(flags_ref[1:2, :], ex1_ref[piece, :], carried)
+        value = jnp.maximum(ex1_ref[piece, :], carried)
         price[0, piece, :] = value.astype(jnp.bfloat16)
         for m in range(rows - 2, 0, -2):
             if not relayed(m, h):
                 p_copy(m, h).start()
         p_copy(1, h).start()
         v1_ref[piece, :] = value
-    keep_one = pltpu.make_async_copy(v1_ref, v1_out, local.at[9])
-    keep_one.start()
-    def add_zero(m, row, first, count):
-        parts = []
-        each = min(step, count)
-        for at in range(first, first + count, each):
-            w = (e0[m, at : at + each, :] * f0[at // step, pl.ds(row, 1), :]).astype(jnp.bfloat16)
-            parts.append(jnp.dot(w, price[m], preferred_element_type=jnp.float32))
-        return parts[0] if len(parts) == 1 else jnp.concatenate(parts, axis=0)
-
-    def gain(slots):
-        for at in range(0, sources, step):
-            total = acc0[at : at + step, :] if 0 not in slots else None
-            for m in slots:
-                part = add_zero(m, flip(group, m, rows), at, step)
-                total = part if total is None else total + part
-            acc0[at : at + step, :] = total
+    def weigh(m):
+        row = flip(group, m, rows)
+        for b in range(blocks):
+            part = e0[m, b * step : (b + 1) * step, :] * f0[b, pl.ds(row, 1), :]
+            wz[m, b * step : (b + 1) * step, :] = part.astype(jnp.bfloat16)
+
+    def sides(m, half):
+        p = price[m, half * half_own : (half + 1) * half_own, :].astype(jnp.float32)
+        t = turned(p)
+        return p, t
+
+    def stacked(a, b):
+        return jnp.concatenate([a, b], axis=0).astype(jnp.bfloat16)
+
+    def times(m, first, many, right):
+        return jnp.dot(wz[m, pl.ds(first, many), :], right, preferred_element_type=jnp.float32)
+
+    def rights(m, half):
+        p = price[m, half * half_own : (half + 1) * half_own, :]
+        t = turned(p)
+        return m, jnp.concatenate([p, t], axis=0), jnp.concatenate([t, p], axis=0)
+
+    def products(pairs, at):
+        upper = lower = None
+        for m, right, left in pairs:
+            a = times(m, at, quarter, right)
+            b = times(m, near + at, quarter, left)
+            upper = a if upper is None else upper + a
+            lower = b if lower is None else lower + b
+        return upper, lower
+
+    def gain_both(slots):
+        pairs = []
+        for m in slots:
+            weigh(m)
+            (pa, ta), (pb, tb) = sides(m, 0), sides(m, 1)
+            pairs.append((m, stacked(mixed(pa, pb), mixed(ta, tb)), stacked(mixed(tb, ta), mixed(pb, pa))))
+        for at in range(0, near, quarter):
+            upper, lower = products(pairs, at)
+            acc0[0, at : at + quarter, :] = mixed(upper, lower)
+            acc0[1, at : at + quarter, :] = mixed(lower, upper)
+
+    def product(pairs, half, at):
+        upper, lower = products(pairs, at)
+        return mixed(lower, upper) if half else mixed(upper, lower)
+
+    def gain(slots, half):
+        pairs = [rights(m, half) for m in slots]
+        for at in range(0, near, quarter):
+            acc0[half, at : at + quarter, :] = acc0[half, at : at + quarter, :] + product(pairs, half, at)
 
     def pass_on(m, h):
         p_copy(m, h).wait_recv()
@@ -489,63 +548,82 @@
 
     direct = [m for m in range(2, rows, 2) if m % 4 == 0 or m == 2]
     other = [m for m in range(2, rows, 2) if m not in direct]
-    for h in range(PARTS):
+    ahead = [m for m in range(3, rows - 2, 2)]
+
+    def pass_all(h):
         for m in reversed(direct):
             pass_on(m, h)
         for m in other:
             if not relayed(m, h):
                 pass_on(m, h)
-        if h == PARTS // 2 - 1:
-            ready_zero()
-            p_core(1).wait_recv()
-            gain([0, 1])
-    gain(direct)
-    for h in range(min(RELAY, PARTS)):
+
+    def finish(half):
+        pairs = [rights(final, half)]
+        here = slice(half * half_own, (half + 1) * half_own)
+        for dy in (1, 0):
+            total = acc0[half, dy * quarter : (dy + 1) * quarter, :] + product(pairs, half, dy * quarter)
+            for s in [s + dy for s in away] + [dy]:
+                part = total[s // 2 * half_own : (s // 2 + 1) * half_own]
+                if s:
+                    far_out0[s, here, :] = part.astype(far_out0.dtype)
+                    last_copy(s, half).start()
+                else:
+                    v0_ref[here, :] = part
+
+    def mid_core(half, early):
+        for m in ahead:
+            p_core(m, half).wait_recv()
+
+        @pl.when(core == 0)
+        def _():
+            if rows > 2:
+                p_core(rows - 1, half).wait_recv()
+            slots = early + ahead + (other[:-1] + [rows - 1] if other else [])
+            if slots:
+                gain(slots, half)
+
+        @pl.when(core == 1)
+        def _():
+            slots = early + ahead + other
+            if slots:
+                gain(slots, half)
+            if rows > 2:
+                p_core(rows - 1, half).wait_recv()
+
+    final = rows - 2 + core if other else rows - 1
+    pass_all(0)
+    ready_zero()
+    for half in range(2):
+        p_core(1, half).wait_recv()
+    gain_both([0, 1])
+    for m in range(2, rows):
+        weigh(m)
+    v1_ref[...] = unpacked(v1_ref[...])
+    keep_one = pltpu.make_async_copy(v1_ref, v1_out, local.at[9])
+    keep_one.start()
+    for h in range(1, PARTS // 2):
+        pass_all(h)
+    gain(direct, 0)
+    for h in range(min(RELAY, PARTS // 2)):
         for m in other:
             pass_on(m, h)
-    ahead = [m for m in range(3, rows - 2, 2)]
-    for m in ahead:
-        p_core(m).wait_recv()
-    if ahead:
-        gain(ahead)
-
-    @pl.when(core == 0)
-    def _():
-        if rows > 2:
-            p_core(rows - 1).wait_recv()
-        if other:
-            gain(other[:-1] + [rows - 1])
-
-    @pl.when(core == 1)
-    def _():
-        if other:
-            gain(other)
-        if rows > 2:
-            p_core(rows - 1).wait_recv()
-
-    if other:
-        final, final_row = rows - 2 + core, flip(group, rows - 2, rows) - core
-    else:
-        final, final_row = rows - 1, flip(group, rows - 1, rows)
-    held = None
-    for s in [s + 1 for s in away] + away + [1, 0]:
-        at = (s % 2) * near + s // 2 * own
-        total = acc0[at : at + own, :] + add_zero(final, final_row, at, own)
-        if s:
-            far_out0[s] = total.astype(far_out0.dtype)
-            for h in range(LAST):
-                last_copy(s, h).start()
-        else:
-            held = total
-    loads[8].wait()
+    pass_all(PARTS // 2)
+    mid_core(0, [])
+    for h in range(PARTS // 2 + 1, PARTS):
+        pass_all(h)
+    finish(0)
+    gain(direct, 1)
+    mid_core(1, [])
+    finish(1)
     for h in range(LAST):
         piece = slice(h * count, (h + 1) * count)
-        carried = held[piece]
         view = far_in0.at[pl.ds(1, cols - 1), pl.ds(h * count, count)]
         remote(view, view, far0_send.at[0], far0_recv.at[h], col_peer(1)).wait_recv()
+        carried = v0_ref[piece, :]
         for s in range(1, cols):
             carried = carried + far_in0[s, piece, :].astype(jnp.float32)
-        v0_ref[piece, :] = settled(flags_ref[0:1, :], ex0_ref[piece, :], carried)
+        v0_ref[piece, :] = jnp.maximum(ex0_ref[piece, :], carried)
+    v0_ref[...] = unpacked(v0_ref[...])
     keep_zero = pltpu.make_async_copy(v0_ref, v0_out, local.at[10])
     keep_zero.start()
 
@@ -578,8 +656,7 @@
     trades = terminal.shape[1]
     width = min(TILE, targets)
     chunks = targets // width
-    step = max(own, min(TILE, sources))
-    blocks = sources // step
+    blocks = 4
     lanes = 128 * (-(-(depth + 3) // 128))
     dma = pltpu.SemaphoreType.DMA
     f32, bf16 = jnp.float32, jnp.bfloat16
@@ -606,7 +683,8 @@
             pltpu.VMEM((cols, own, lanes), bf16),
             pltpu.VMEM((rows, lanes, own), bf16),
             pltpu.VMEM((sources, lanes), bf16),
-            pltpu.VMEM((sources, lanes), bf16),
+            pltpu.VMEM((2, 2, sources // 4, lanes), bf16),
+            pltpu.VMEM((rows, sources, own), bf16),
             pltpu.VMEM((chunks, lanes, width), bf16),
             pltpu.VMEM((cols, chunks, own, width), f32),
             pltpu.VMEM((rows, sources, own), f32),
@@ -621,7 +699,7 @@
             pltpu.VMEM((rows // 2, rows, own), f32),
             pltpu.VMEM((rows, own, trades), bf16),
             piece,
-            pltpu.VMEM((sources, trades), f32),
+            pltpu.VMEM((2, sources // 2, trades), f32),
             *[piece] * 4,
             *[slim] * 2,
             dma((1,)),
@@ -630,7 +708,7 @@
             dma((4,)),
             *[dma((1,))] * 7,
             dma((PARTS * max(1, rows // 2 - 1),)),
-            dma((rows // 2,)),
+            dma((rows,)),
             dma((1,)),
             dma((CUTS * (cols // 2),)),
             dma((1,)),

time: 33.3 us -> 32.9 us (0.988)
  Pallas kernels: 32.5 us -> 32.1 us
    pallas_call x1, Pallas kernels: 31.8 us -> 31.4 us  [shards(): pl.pallas_call(functools.partial(body, rows, cols), out_shape=(pltpu.VMEM...]
where the time goes in v6:
time: 32.9 us; the launch traced here: 32.7 us
  Pallas kernels  32.1 us (98%)
  between operations  0.64 us (2%)
    pallas_call x1, Pallas kernels, shards(): pl.pallas_call(functools.partial(body, rows, cols), out_shape=(pltpu.VMEM...  31.4 us
    pallas_call x1, Pallas kernels, handed(): pl.pallas_call(hand, out_shape=(out, out), in_specs=[here, here], out_spe...  0.72 us

profile of v6, /device:TPU:0, one launch (start us, length us, event | category | flops | bytes accessed | tf_op | source)
XLA Modules:
  0.0 32.7 jit_solution(5476284500820197475)
XLA Ops:
  0.6 31.4 %shard_map.104 = (f32[256,128]{1,0:T(8,128)S(1)}, f32[256,128]{1,0:T(8,128)S(1)}) custom-call(f32[64,1024]{1,0:T(8,128)} %bitcast.6, f32[64,256]{1,0:T(8,128)} %bitcast.7, f32[64,2048]{1,0:T(8,128)} %bitcast.5, f32[1,64]{1,0:T(1,128)} %bitcast.8, f32[1,64]{1,0:T(1,128)} %bitcast.9, bf16[2048,128]{1,0:T(8,128)(2,1)} %terminal_hbm.1, f32[256,128]{1,0:T(8,128)} %ex1_hbm.1, ...), custom_call_target="tpu_custom_call" | custom-call | tf_op jit(solution)/shard_map/pallas_call | solution.py:668
  32.0 0.7 %shard_map.105 = (f32[256,128]{1,0:T(8,128)}, f32[256,128]{1,0:T(8,128)}) custom-call(f32[256,128]{1,0:T(8,128)S(1)} %get-tuple-element.4.a, f32[256,128]{1,0:T(8,128)S(1)} %get-tuple-element.5.b), custom_call_target="tpu_custom_call" | custom-call | tf_op jit(solution)/shard_map/pallas_call | solution.py:739

commit v7 on v6

--- a/solution.py
+++ b/solution.py
@@ -557,8 +557,8 @@
             if not relayed(m, h):
                 pass_on(m, h)
 
-    def finish(half):
-        pairs = [rights(final, half)]
+    def finish(half, slots):
+        pairs = [rights(m, half) for m in slots]
         here = slice(half * half_own, (half + 1) * half_own)
         for dy in (1, 0):
             total = acc0[half, dy * quarter : (dy + 1) * quarter, :] + product(pairs, half, dy * quarter)
@@ -570,27 +570,11 @@
                 else:
                     v0_ref[here, :] = part
 
-    def mid_core(half, early):
-        for m in ahead:
+    def take_core(slots, half):
+        for m in slots:
             p_core(m, half).wait_recv()
 
-        @pl.when(core == 0)
-        def _():
-            if rows > 2:
-                p_core(rows - 1, half).wait_recv()
-            slots = early + ahead + (other[:-1] + [rows - 1] if other else [])
-            if slots:
-                gain(slots, half)
-
-        @pl.when(core == 1)
-        def _():
-            slots = early + ahead + other
-            if slots:
-                gain(slots, half)
-            if rows > 2:
-                p_core(rows - 1, half).wait_recv()
-
-    final = rows - 2 + core if other else rows - 1
+    ends = other + ([rows - 1] if rows > 2 else [])
     pass_all(0)
     ready_zero()
     for half in range(2):
@@ -608,13 +592,16 @@
         for m in other:
             pass_on(m, h)
     pass_all(PARTS // 2)
-    mid_core(0, [])
+    take_core(ahead, 0)
     for h in range(PARTS // 2 + 1, PARTS):
         pass_all(h)
-    finish(0)
+    if ahead:
+        gain(ahead, 0)
+    take_core([rows - 1], 0)
+    finish(0, ends)
     gain(direct, 1)
-    mid_core(1, [])
-    finish(1)
+    take_core(ahead + [rows - 1], 1)
+    finish(1, ahead + ends)
     for h in range(LAST):
         piece = slice(h * count, (h + 1) * count)
         view = far_in0.at[pl.ds(1, cols - 1), pl.ds(h * count, count)]

time: 32.9 us -> 32.7 us (level)
  no operation moved by 1% of the time
where the time goes in v7:
time: 32.7 us; the launch traced here: 32.5 us
  Pallas kernels  31.9 us (98%)
  between operations  0.64 us (2%)
    pallas_call x1, Pallas kernels, shards(): pl.pallas_call(functools.partial(body, rows, cols), out_shape=(pltpu.VMEM...  31.2 us
    pallas_call x1, Pallas kernels, handed(): pl.pallas_call(hand, out_shape=(out, out), in_specs=[here, here], out_spe...  0.72 us

profile of v7, /device:TPU:0, one launch (start us, length us, event | category | flops | bytes accessed | tf_op | source)
XLA Modules:
  0.0 32.5 jit_solution(9990202991526341613)
XLA Ops:
  0.6 31.2 %shard_map.104 = (f32[256,128]{1,0:T(8,128)S(1)}, f32[256,128]{1,0:T(8,128)S(1)}) custom-call(f32[64,1024]{1,0:T(8,128)} %bitcast.6, f32[64,256]{1,0:T(8,128)} %bitcast.7, f32[64,2048]{1,0:T(8,128)} %bitcast.5, f32[1,64]{1,0:T(1,128)} %bitcast.8, f32[1,64]{1,0:T(1,128)} %bitcast.9, bf16[2048,128]{1,0:T(8,128)(2,1)} %terminal_hbm.1, f32[256,128]{1,0:T(8,128)} %ex1_hbm.1, ...), custom_call_target="tpu_custom_call" | custom-call | tf_op jit(solution)/shard_map/pallas_call | solution.py:655
  31.8 0.7 %shard_map.105 = (f32[256,128]{1,0:T(8,128)}, f32[256,128]{1,0:T(8,128)}) custom-call(f32[256,128]{1,0:T(8,128)S(1)} %get-tuple-element.4.a, f32[256,128]{1,0:T(8,128)S(1)} %get-tuple-element.5.b), custom_call_target="tpu_custom_call" | custom-call | tf_op jit(solution)/shard_map/pallas_call | solution.py:726

commit v8 on v7

--- a/solution.py
+++ b/solution.py
@@ -297,7 +297,7 @@
 
     def take_q(s):
         q_copy(s, col_peer(1)).wait_recv()
-        q1[s] = upright(q1t[s].astype(jnp.float32), lanes)
+        q1[s] = upright(q1t[s], lanes)
 
     stats_one(0)
     loads[4].wait()
@@ -454,7 +454,7 @@
         if m % 2:
             src, peer, recv = price.at[m - 1, piece], col_peer(1), pc_recv.at[h * 2 // PARTS * line + m // 2]
         else:
-            recv = p_recv.at[h * (rows // 2 - 1) + m // 2 - 1]
+            recv = p_recv.at[PARTS + h * (rows // 2) + m // 2 if relayed(m, h) else h]
             src, peer = (price.at[m - 2, piece], row_peer(2)) if relayed(m, h) else (price.at[0, piece], row_peer(m))
         return remote(src, price.at[m, piece], p_send.at[0], recv, peer)
 
@@ -530,7 +530,8 @@
             acc0[half, at : at + quarter, :] = acc0[half, at : at + quarter, :] + product(pairs, half, at)
 
     def pass_on(m, h):
-        p_copy(m, h).wait_recv()
+        if relayed(m, h):
+            p_copy(m, h).wait_recv()
         if m + 2 < rows and relayed(m + 2, h) and m % 4 == 0:
             p_copy(m + 2, h).start()
         p_copy(m + 1, h).start()
@@ -551,6 +552,8 @@
     ahead = [m for m in range(3, rows - 2, 2)]
 
     def pass_all(h):
+        view = price.at[pl.ds(0, sum(not relayed(m, h) for m in range(2, rows, 2))), pl.ds(h * size, size)]
+        remote(view, view, p_send.at[0], p_recv.at[h], col_peer(1)).wait_recv()
         for m in reversed(direct):
             pass_on(m, h)
         for m in other:
@@ -583,7 +586,7 @@
     for m in range(2, rows):
         weigh(m)
     v1_ref[...] = unpacked(v1_ref[...])
-    keep_one = pltpu.make_async_copy(v1_ref, v1_out, local.at[9])
+    keep_one = pltpu.make_async_copy(v1_ref, v1_out, local.at[0])
     keep_one.start()
     for h in range(1, PARTS // 2):
         pass_all(h)
@@ -611,7 +614,7 @@
             carried = carried + far_in0[s, piece, :].astype(jnp.float32)
         v0_ref[piece, :] = jnp.maximum(ex0_ref[piece, :], carried)
     v0_ref[...] = unpacked(v0_ref[...])
-    keep_zero = pltpu.make_async_copy(v0_ref, v0_out, local.at[10])
+    keep_zero = pltpu.make_async_copy(v0_ref, v0_out, local.at[1])
     keep_zero.start()
 
     y_copy.wait_send()
@@ -694,7 +697,7 @@
             dma((1,)),
             dma((4,)),
             *[dma((1,))] * 7,
-            dma((PARTS * max(1, rows // 2 - 1),)),
+            dma((PARTS + max(0, RELAY - 1) * (rows // 2) + rows // 2,)),
             dma((rows,)),
             dma((1,)),
             dma((CUTS * (cols // 2),)),
@@ -702,7 +705,7 @@
             dma((PARTS * max(1, cols // 2 - 1),)),
             *[dma((1,))] * 3,
             dma((LAST,)),
-            dma((11,)),
+            dma((9,)),
             pltpu.SemaphoreType.REGULAR((max(1, rows // 2 - 1),)),
         ],
         compiler_params=pltpu.CompilerParams(

time: 32.7 us -> 32.7 us (level)
  no operation moved by 1% of the time
where the time goes in v8:
time: 32.7 us; the launch traced here: 32.6 us
  Pallas kernels  31.9 us (98%)
  between operations  0.64 us (2%)
    pallas_call x1, Pallas kernels, shards(): pl.pallas_call(functools.partial(body, rows, cols), out_shape=(pltpu.VMEM...  31.2 us
    pallas_call x1, Pallas kernels, handed(): pl.pallas_call(hand, out_shape=(out, out), in_specs=[here, here], out_spe...  0.72 us

profile of v8, /device:TPU:0, one launch (start us, length us, event | category | flops | bytes accessed | tf_op | source)
XLA Modules:
  0.0 32.6 jit_solution(3422767593634696522)
XLA Ops:
  0.6 31.2 %shard_map.104 = (f32[256,128]{1,0:T(8,128)S(1)}, f32[256,128]{1,0:T(8,128)S(1)}) custom-call(f32[64,1024]{1,0:T(8,128)} %bitcast.6, f32[64,256]{1,0:T(8,128)} %bitcast.7, f32[64,2048]{1,0:T(8,128)} %bitcast.5, f32[1,64]{1,0:T(1,128)} %bitcast.8, f32[1,64]{1,0:T(1,128)} %bitcast.9, bf16[2048,128]{1,0:T(8,128)(2,1)} %terminal_hbm.1, f32[256,128]{1,0:T(8,128)} %ex1_hbm.1, ...), custom_call_target="tpu_custom_call" | custom-call | tf_op jit(solution)/shard_map/pallas_call | solution.py:658
  31.8 0.7 %shard_map.105 = (f32[256,128]{1,0:T(8,128)}, f32[256,128]{1,0:T(8,128)}) custom-call(f32[256,128]{1,0:T(8,128)S(1)} %get-tuple-element.4.a, f32[256,128]{1,0:T(8,128)S(1)} %get-tuple-element.5.b), custom_call_target="tpu_custom_call" | custom-call | tf_op jit(solution)/shard_map/pallas_call | solution.py:729
